TPU v7x, 32 devices: a whole 2x2x4 slice. The times are simulated.
32 devices in a mesh: comp: 2 (over x), tile: 16 (over z, y, core).
Axes of the slice: x: 2, y: 2, z: 4, core: 2. Of those that a mesh axis runs over, the one named last changes fastest.
Arguments:
- state: float32 [2, 16, 512, 1024], P('comp', None, 'tile'), may hold values from -6 to 6
- kappa: float32 [2, 16], P('comp'), may hold values from 0.02 to 0.24
- col_mix: float32 [2, 16, 16], P('comp'), may hold values from -1.5 to 1.5
- surface_mask: int32 [2, 512, 1024], P('comp', 'tile'), may hold values 0 or 1
- lagged_flux: float32 [8, 512, 1024], P(None, 'tile'), may hold values from -6 to 6
- a2l_src: int32 [16, 16, 4], P(None, 'tile'), may hold values from 0 to 255
- a2l_dst: int32 [16, 16, 4], P('tile'), may hold values from 0 to 255
- a2l_count: int32 [16, 16], P('tile'), may hold values from 0 to 4, as said below
- a2l_weight: bfloat16 [16, 16, 4, 128, 128], P('tile'), may hold values from 0.049804688 to 1
- l2a_src: int32 [16, 16, 4], P(None, 'tile'), may hold values from 0 to 255
- l2a_dst: int32 [16, 16, 4], P('tile'), may hold values from 0 to 255
- l2a_count: int32 [16, 16], P(None, 'tile'), may hold values from 0 to 4, as said below
- l2a_weight: bfloat16 [16, 16, 4, 128, 128], P(None, 'tile'), may hold values from 0.049804688 to 1
Outputs:
- new_state: float32 [2, 16, 512, 1024], P('comp', None, 'tile')
- fluxes: float32 [2, 8, 512, 1024], P('comp', None, 'tile')
Inputs may be any that keep to these rules, and one draw needn't show every extreme that they name: `a2l_count`: for each destination tile, some source tile has exactly 4 live slots. `l2a_count`: for each destination tile, some source tile has exactly 4 live slots.
All inputs are finite; a program needn't handle non-finite values. No bound on the sum of `surface_mask` on one device may be relied on, other than what follows from the above.
Results may differ from a plain program's by a relative error of at most 0.0008.
Values may be sent and summed in bfloat16 or wider, within the bound.
No kernel may reach another device: no remote copies, remote signals or barrier semaphores. Data moves between devices by JAX's collectives and lax.ppermute only.
A program may use at most 128 MiB of HBM per device.

v0:
```python
import jax
import jax.numpy as jnp
from jax import lax
from jax.sharding import PartitionSpec as P

NF = 8
BLK = 128
CAP = 4
NSUB = 2


def from_behind(value, axis, steps):
    count = lax.axis_size(axis)
    pairs = [(source, (source + steps) % count) for source in range(count)]
    return lax.ppermute(value, axis, pairs)


def extended(array, sides, width):
    for axis, dim in sides:
        size, length = (lax.axis_size(axis), array.shape[dim])
        up = [(i, (i + 1) % size) for i in range(size - 1)]
        down = [(j, i) for i, j in up]
        last = lax.slice_in_dim(array, length - width, length, axis=dim)
        initial = lax.slice_in_dim(array, 0, width, axis=dim)
        before = lax.ppermute(last, axis, up)
        after = lax.ppermute(initial, axis, down)
        array = jnp.concatenate([before, array, after], axis=dim)
    return array


def pick_blocks(blocks, indices, tile_count):
    picked = jnp.take(blocks, indices.reshape(-1), axis=1)
    return picked.reshape(NF, tile_count, CAP, BLK)


def live_mask(counts):
    return (jnp.arange(CAP, dtype=jnp.int32)[None, :] < counts[:, None]).astype(jnp.float32)


def weigh_blocks(picked, weights, counts):
    live_slots = live_mask(counts)
    contrib = jnp.einsum("fsck,sckm->fscm", picked, weights, preferred_element_type=jnp.float32)
    contrib = contrib * live_slots[None, :, :, None]
    column = jnp.sum(weights, axis=2, dtype=jnp.float32) * live_slots[:, :, None]
    return (contrib, column[None])


def combine_blocks(contrib, column, index_dst, nblocks):
    onehot = (
        index_dst.reshape(-1)[:, None] == jnp.arange(nblocks, dtype=jnp.int32)[None, :]
    ).astype(jnp.float32)
    entries = index_dst.shape[0] * index_dst.shape[1]
    numerator = jnp.einsum(
        "fem,eb->fbm", contrib.reshape(NF, entries, BLK), onehot, precision=lax.Precision.HIGHEST
    )
    denominator = jnp.einsum(
        "em,eb->bm", column.reshape(entries, BLK), onehot, precision=lax.Precision.HIGHEST
    )
    return numerator / jnp.maximum(denominator, 1.0)[None]


def stencil_sum(padded, center):
    return (
        padded[:, 2:] + padded[:, :-2] + jnp.roll(center, 1, axis=2) + jnp.roll(center, -1, axis=2)
    )


def per_device(
    state,
    kappa,
    col_mix,
    surface_mask,
    lagged_flux,
    a2l_src,
    a2l_dst,
    a2l_count,
    a2l_weight,
    l2a_src,
    l2a_dst,
    l2a_count,
    l2a_weight,
):
    fields = state[0]
    levels, row_count, row_cells = fields.shape
    nblocks = row_count * row_cells // BLK
    tile_count = lax.axis_size("tile")
    land_side = lax.axis_index("comp") == 1
    forcing = fields[:NF].astype(jnp.bfloat16).reshape(NF, nblocks, BLK)
    picked = pick_blocks(forcing, a2l_src[:, 0, :], tile_count)
    shipped = lax.all_to_all(picked, "tile", split_axis=1, concat_axis=1, tiled=True)
    arrived = from_behind(shipped, "comp", 1)
    contrib, column = weigh_blocks(arrived, a2l_weight[0], a2l_count[0])
    remapped_forcing = combine_blocks(contrib, column, a2l_dst[0], nblocks).reshape(
        NF, row_count, row_cells
    )
    rates = kappa[0][:, None, None]
    widened = extended(fields, (("tile", 1),), NSUB)
    global_row = (
        lax.axis_index("tile") * row_count
        - NSUB
        + jnp.arange(row_count + 2 * NSUB, dtype=jnp.int32)
    )
    inside = ((global_row >= 0) & (global_row < row_count * tile_count)).astype(jnp.float32)[
        None, :, None
    ]
    for substep in range(NSUB):
        padded = jnp.pad(widened, ((0, 0), (1, 1), (0, 0)))
        beside_all = stencil_sum(padded, widened)
        widened = (widened + rates * (beside_all - 4.0 * widened)) * inside
    diffused = widened[:, NSUB : NSUB + row_count]
    incoming = jnp.where(land_side, remapped_forcing, lagged_flux + remapped_forcing)
    land_frac = surface_mask[0].astype(jnp.float32)[None]
    mixing = jnp.einsum("lm,mrw->lrw", col_mix[0], diffused, precision=lax.Precision.HIGHEST)
    surface = land_frac * incoming - (1.0 - land_frac) * 0.5 * diffused[:NF]
    new_state = diffused + 0.5 * jnp.tanh(mixing)
    new_state = new_state.at[:NF].add(surface)
    flux_local = land_frac * jnp.tanh(new_state[:NF] - incoming)
    flux_blocks16 = flux_local.astype(jnp.bfloat16).reshape(NF, nblocks, BLK)
    contrib, column = weigh_blocks(
        pick_blocks(flux_blocks16, l2a_src[:, 0, :], tile_count), l2a_weight[:, 0], l2a_count[:, 0]
    )
    shipped = (
        lax.all_to_all(
            contrib.astype(jnp.bfloat16), "tile", split_axis=1, concat_axis=1, tiled=True
        ).astype(contrib.dtype),
        lax.all_to_all(
            column.astype(jnp.bfloat16), "tile", split_axis=1, concat_axis=1, tiled=True
        ).astype(column.dtype),
    )
    got_contrib, got_column = (
        from_behind(shipped[0].astype(jnp.bfloat16), "comp", 1).astype(jnp.float32),
        from_behind(shipped[1].astype(jnp.bfloat16), "comp", 1).astype(jnp.float32),
    )
    remapped_flux = combine_blocks(got_contrib, got_column, l2a_dst[0], nblocks).reshape(
        NF, row_count, row_cells
    )
    fluxes = jnp.where(land_side, flux_local + remapped_flux, remapped_flux)
    return (new_state[None], fluxes[None])


def solution(mesh):
    return jax.shard_map(
        per_device,
        mesh=mesh,
        in_specs=(
            P("comp", None, "tile", None),
            P("comp", None),
            P("comp", None, None),
            P("comp", "tile", None),
            P(None, "tile", None),
            P(None, "tile", None),
            P("tile", None, None),
            P("tile", None),
            P("tile", None, None, None, None),
            P(None, "tile", None),
            P("tile", None, None),
            P(None, "tile"),
            P(None, "tile", None, None, None),
        ),
        out_specs=(P("comp", None, "tile", None), P("comp", None, "tile", None)),
        check_vma=False,
    )
```

profile of v0, /device:TPU:0, one launch (start us, length us, event | category | flops | bytes accessed | tf_op | source)
XLA Modules:
  0.0 89.9 jit_solution(1522823537247913568)
XLA Ops:
  0.7 2.8 %copy.101 = f32[1,16,32,1024]{3,1,2,0:T(8,128)S(1)} copy(f32[1,16,32,1024]{3,2,1,0:T(8,128)} %param.17) | data formatting | bytes 4194304 | tf_op args[0]
  3.5 0.7 fusion.56
  4.2 1.4 %collective-permute-start.1 = (f32[16,2,1024]{2,0,1:T(8,128)}, f32[16,2,1024]{2,0,1:T(8,128)}, u32[]{:S(2)}, u32[]{:S(2)}) collective-permute-start(f32[16,2,1024]{2,0,1:T(8,128)} %get-tuple-element.34), channel_id=1, source_target_pairs={{1,0},{2,1},{3,2},{4,3},{5,4},{6,5},{7,6},{8,7},{9,8},{10,9},{11,1... | collective-permute-start | bytes 393224 | tf_op jit(solution)/shard_map/ppermute | solution.py:26
  5.6 3.7 %collective-permute-start = (f32[16,2,1024]{2,0,1:T(8,128)}, f32[16,2,1024]{2,0,1:T(8,128)}, u32[]{:S(2)}, u32[]{:S(2)}) collective-permute-start(f32[16,2,1024]{2,0,1:T(8,128)} %get-tuple-element.33), channel_id=1, source_target_pairs={{0,1},{1,2},{2,3},{3,4},{4,5},{5,6},{6,7},{7,8},{8,9},{9,10},{10,1... | collective-permute-start | bytes 393224 | tf_op jit(solution)/shard_map/ppermute | solution.py:25
  9.3 1.3 %slice.171 = bf16[1,8,32,1024]{3,2,1,0:T(8,128)(2,1)S(1)} slice(f32[1,16,32,1024]{3,2,1,0:T(8,128)} %param.17), slice={[0:1], [0:8], [0:32], [0:1024]} | slice | bytes 1048576 | tf_op jit(solution)/shard_map/slice | solution.py:88
  10.8 0.2 convert_element_type.83
  11.1 0.3 copy.61
  11.4 0.6 gather_fusion
  12.1 0.8 broadcast_select_fusion.1
  12.9 7.4 %all-to-all-start = ((bf16[8,16,4,128]{3,0,2,1:T(8,128)(2,1)}), bf16[8,16,4,128]{3,0,2,1:T(8,128)(2,1)S(1)}, u32[]{:S(2)}, u32[]{:S(2)}) async-start(bf16[8,16,4,128]{3,0,2,1:T(8,128)(2,1)} %bitcast.9), calls=%async_computation | async-start | bytes 262144 | tf_op jit(solution)/shard_map/all_to_all | solution.py:90
  20.6 0.5 compare_and_fusion
  21.1 2.1 %convert_reduce_fusion.1 = f32[16,4,128]{2,1,0:T(4,128)S(1)} fusion(bf16[1,16,4,128,128]{4,3,2,1,0:T(8,128)(2,1)} %param.25), kind=kLoop, calls=%fused_computation.3 | loop fusion | flops 2088960 | bytes 2129920 | tf_op jit(solution)/shard_map/reduce_sum | solution.py:44
  23.5 2.1 %convert_reduce_fusion = f32[16,4,128]{2,1,0:T(4,128)S(1)} fusion(bf16[16,1,4,128,128]{4,3,2,1,0:T(8,128)(2,1)} %param.29), kind=kLoop, calls=%fused_computation.2 | loop fusion | flops 2088960 | bytes 2129920 | tf_op jit(solution)/shard_map/reduce_sum | solution.py:44
  25.7 0.7 fusion.41
  26.4 0.4 convolution_maximum_fusion.1
  26.8 0.6 pad_clamp_fusion
  27.4 1.2 %pad_maximum_fusion = f32[16,36,1024]{2,0,1:T(8,128)S(1)} fusion(f32[16,2,1024]{2,0,1:T(8,128)} %collective-permute-done.1, f32[16,32,1024]{2,0,1:T(8,128)S(1)} %bitcast.78, f32[16,2,1024]{2,0,1:T(8,128)} %collective-permute-done), kind=kLoop, calls=%fused_computation.22 | loop fusion | flops 1179648 | bytes 4718592 | tf_op jit(solution)/shard_map/concatenate | solution.py:27
  28.6 0.9 %fusion.54 = (f32[16,36,1023]{2,0,1:T(8,128)S(1)}, f32[16,36,1023]{2,0,1:T(8,128)S(1)}) fusion(f32[16,36,1024]{2,0,1:T(8,128)S(1)} %pad_maximum_fusion), kind=kLoop, calls=%fused_computation.81 | loop fusion | bytes 9427968 | tf_op jit(solution)/shard_map/jit(_roll_static)/slice | solution.py:64
  29.6 0.2 fusion.55
  29.7 1.8 %fusion.6 = f32[16,36,1024]{2,0,1:T(8,128)S(1)} fusion(f32[16,36,1024]{2,0,1:T(8,128)S(1)} %pad_maximum_fusion, f32[16,36,1023]{2,0,1:T(8,128)S(1)} %get-tuple-element.30, f32[16,36,1]{2,0,1:T(8,128)S(1)} %get-tuple-element.32, f32[16,36,1]{2,0,1:T(8,128)S(1)} %get-tuple-element.31, f32[16,36,1023]{2,0,1:T(8,128)S(1)} %get-tuple-element.29, ...), kind=kLoop, calls=%fused_computation.14 | loop fusion | flops 5898240 | bytes 9437392 | tf_op jit(solution)/shard_map/mul | solution.py:109
  31.5 0.9 %fusion.52 = (f32[16,36,1023]{2,0,1:T(8,128)S(1)}, f32[16,36,1023]{2,0,1:T(8,128)S(1)}) fusion(f32[16,36,1024]{2,0,1:T(8,128)S(1)} %fusion.6), kind=kLoop, calls=%fused_computation.79 | loop fusion | bytes 9427968 | tf_op jit(solution)/shard_map/jit(_roll_static)/slice | solution.py:64
  32.5 0.2 fusion.53
  32.6 2.8 %fusion.13 = f32[16,36,1024]{2,0,1:T(8,128)} fusion(f32[16,36,1024]{2,0,1:T(8,128)S(1)} %fusion.6, f32[16,36,1023]{2,0,1:T(8,128)S(1)} %get-tuple-element.26, f32[16,36,1]{2,0,1:T(8,128)S(1)} %get-tuple-element.28, f32[16,36,1]{2,0,1:T(8,128)S(1)} %get-tuple-element.27, f32[16,36,1023]{2,0,1:T(8,128)S(1)} %get-tuple-element.25, f32[36]{0:T(128)S(1)} %and_convert_fusion, ...), kind=kLoop, calls=%fused_computation.21 | loop fusion | flops 5898240 | bytes 9437392 | tf_op jit(solution)/shard_map/mul | solution.py:109
  35.5 6.1 %all-to-all-start.2 = ((bf16[1,16,4,128]{3,2,0,1:T(4,128)(2,1)}), bf16[1,16,4,128]{3,2,0,1:T(4,128)(2,1)}, u32[]{:S(2)}, u32[]{:S(2)}) async-start(bf16[1,16,4,128]{3,2,0,1:T(4,128)(2,1)} %fusion.41), calls=%async_computation.2 | async-start | bytes 32768 | tf_op jit(solution)/shard_map/all_to_all | solution.py:126
  41.5 1.6 %collective-permute-start.2 = (bf16[8,16,4,128]{3,0,2,1:T(8,128)(2,1)S(1)}, bf16[8,16,4,128]{3,0,2,1:T(8,128)(2,1)S(1)}, u32[]{:S(2)}, u32[]{:S(2)}) collective-permute-start(bf16[8,16,4,128]{3,0,2,1:T(8,128)(2,1)S(1)} %all-to-all-done), channel_id=1, source_target_pairs={{0,16},{16,0},{1,17},{17,1},{2,18},{18,2},{3,19},{19,3},{4,20},{20... | collective-permute-start | bytes 393224 | tf_op jit(solution)/shard_map/ppermute | solution.py:15
  43.1 4.4 %slice_add_fusion = f32[16,32,1024]{2,0,1:T(8,128)S(1)} fusion(f32[16,36,1024]{2,0,1:T(8,128)} %fusion.13, f32[1,16,16]{2,1,0:T(8,128)S(1)} %copy-done), kind=kOutput, calls=%fused_computation.23 | convolution fusion | flops 101711872 | bytes 6554624 | tf_op jit(solution)/shard_map/lm,mrw->lrw/dot_general | solution.py:113
  47.5 2.2 %fusion.20 = f32[16,4,8,128]{3,2,1,0:T(8,128)S(1)} fusion(bf16[8,16,4,128]{3,0,2,1:T(8,128)(2,1)S(1)} %collective-permute-done.2, bf16[1,16,4,128,128]{4,3,2,1,0:T(8,128)(2,1)} %param.25, f32[16,4]{1,0:T(8,128)S(1)} %fusion.49), kind=kOutput, calls=%fused_computation.35 | convolution fusion | flops 16842752 | bytes 2490624 | tf_op jit(solution)/shard_map/fsck,sckm->fscm/dot_general | solution.py:42
  49.7 1.7 %fusion.19 = f32[8,256,128]{2,1,0:T(8,128)} fusion(f32[256,128]{1,0:T(8,128)S(1)} %convolution_maximum_fusion.1, f32[8,64,128]{2,0,1:T(8,128)S(1)} %bitcast.81, s32[64]{0:T(128)S(1)} %eq.34), kind=kOutput, calls=%fused_computation.34 | convolution fusion | flops 201605120 | bytes 1442048 | tf_op jit(solution)/shard_map/fem,eb->fbm/dot_general | solution.py:53
  51.4 1.4 %reshape.195 = f32[8,32,1024]{2,1,0:T(8,128)S(1)} reshape(f32[8,256,128]{2,1,0:T(8,128)} %fusion.19) | data formatting | bytes 2097152 | tf_op jit(solution)/shard_map/reshape | solution.py:93
  52.8 4.5 %fusion.51 = (bf16[8,32,1024]{2,0,1:T(8,128)(2,1)}, f32[8,32,1024]{2,0,1:T(8,128)}) fusion(f32[16,36,1024]{2,0,1:T(8,128)} %fusion.13, f32[32,1024]{1,0:T(8,128)S(1)} %multiply_bitcast_fusion, f32[8,32,1024]{2,1,0:T(8,128)} %param.21, f32[8,32,1024]{2,1,0:T(8,128)S(1)} %reshape.195, pred[]{:T(512)S(6)} %eq.33, f32[16,32,1024]{2,0,1:T(8,128)S(1)} %slice_add_fusion, ...), kind=kLoop, calls=%fused_computation.78 | loop fusion | flops 2359296 | bytes 6029313 | tf_op jit(solution)/shard_map/convert_element_type | solution.py:118
  57.3 1.8 %gather_fusion.1 = bf16[64,8,128]{2,1,0:T(8,128)(2,1)S(1)} fusion(bf16[8,256,128]{2,0,1:T(8,128)(2,1)} %bitcast.79, s32[1024]{0:T(1024)} %pad_clamp_fusion), kind=kCustom, calls=%fused_computation.1.clone | custom fusion | bytes 262400 | tf_op jit(solution)/shard_map/jit(_take)/gather | solution.py:32
  59.1 0.7 broadcast_select_fusion
  59.8 2.9 %fusion.29 = bf16[8,16,4,128]{3,0,2,1:T(8,128)(2,1)} fusion(bf16[8,16,4,128]{3,0,2,1:T(8,128)(2,1)S(1)} %bitcast.80, bf16[16,1,4,128,128]{4,3,2,1,0:T(8,128)(2,1)} %param.29, f32[16,4]{1,0:T(8,128)S(1)} %fusion.50), kind=kOutput, calls=%fused_computation.38 | convolution fusion | flops 16908288 | bytes 2359552 | tf_op jit(solution)/shard_map/fsck,sckm->fscm/dot_general | solution.py:42
  62.7 6.0 %all-to-all-start.1 = ((bf16[8,16,4,128]{3,0,2,1:T(8,128)(2,1)}), bf16[8,16,4,128]{3,0,2,1:T(8,128)(2,1)}, u32[]{:S(2)}, u32[]{:S(2)}) async-start(bf16[8,16,4,128]{3,0,2,1:T(8,128)(2,1)} %fusion.29), calls=%async_computation.1 | async-start | bytes 262144 | tf_op jit(solution)/shard_map/all_to_all | solution.py:123
  68.7 1.2 %collective-permute-start.4 = (bf16[1,16,4,128]{3,2,0,1:T(4,128)(2,1)}, bf16[1,16,4,128]{3,2,0,1:T(4,128)(2,1)S(1)}, u32[]{:S(2)}, u32[]{:S(2)}) collective-permute-start(bf16[1,16,4,128]{3,2,0,1:T(4,128)(2,1)} %all-to-all-done.2), channel_id=1, source_target_pairs={{0,16},{16,0},{1,17},{17,1},{2,18},{18,2},{3,19},{19,3},{4,20},{20... | collective-permute-start | bytes 49160 | tf_op jit(solution)/shard_map/ppermute | solution.py:15
  70.1 2.6 %collective-permute-done.4 = bf16[1,16,4,128]{3,2,0,1:T(4,128)(2,1)S(1)} collective-permute-done((bf16[1,16,4,128]{3,2,0,1:T(4,128)(2,1)}, bf16[1,16,4,128]{3,2,0,1:T(4,128)(2,1)S(1)}, u32[]{:S(2)}, u32[]{:S(2)}) %collective-permute-start.4) | collective-permute-done | bytes 16416 | tf_op jit(solution)/shard_map/ppermute | solution.py:15
  72.8 0.6 copy-done.3
  73.4 1.0 %convolution_maximum_fusion = f32[256,128]{1,0:T(8,128)S(1)} fusion(bf16[64,128]{1,0:T(8,128)(2,1)} %bitcast.83, s32[64]{0:T(128)S(1)} %eq.38), kind=kOutput, calls=%fused_computation.39 | convolution fusion | flops 4243456 | bytes 147712 | tf_op jit(solution)/shard_map/em,eb->bm/dot_general | solution.py:56
  74.4 1.3 %copy.102 = f32[1,16,32,1024]{3,1,2,0:T(8,128)} copy(f32[1,16,32,1024]{3,1,2,0:T(8,128)S(1)} %bitcast.76) | data formatting | bytes 4194304
  75.7 1.0 %all-to-all-done.1 = bf16[8,16,4,128]{3,0,2,1:T(8,128)(2,1)} async-done(((bf16[8,16,4,128]{3,0,2,1:T(8,128)(2,1)}), bf16[8,16,4,128]{3,0,2,1:T(8,128)(2,1)}, u32[]{:S(2)}, u32[]{:S(2)}) %all-to-all-start.1) | async-done | bytes 131104 | tf_op jit(solution)/shard_map/all_to_all | solution.py:123
  76.7 1.1 %collective-permute-start.3 = (bf16[8,16,4,128]{3,0,2,1:T(8,128)(2,1)}, bf16[8,16,4,128]{3,0,2,1:T(8,128)(2,1)S(1)}, u32[]{:S(2)}, u32[]{:S(2)}) collective-permute-start(bf16[8,16,4,128]{3,0,2,1:T(8,128)(2,1)} %all-to-all-done.1), channel_id=1, source_target_pairs={{0,16},{16,0},{1,17},{17,1},{2,18},{18,2},{3,19},{19,3},{4,20},{20... | collective-permute-start | bytes 393224 | tf_op jit(solution)/shard_map/ppermute | solution.py:15
  77.8 4.5 %bitcast_dynamic-update-slice_fusion = f32[1,16,32,1024]{3,1,2,0:T(8,128)} fusion(f32[1,16,32,1024]{3,1,2,0:T(8,128)} %copy.102, f32[16,36,1024]{2,0,1:T(8,128)} %fusion.13, f32[32,1024]{1,0:T(8,128)S(1)} %multiply_bitcast_fusion, f32[8,32,1024]{2,1,0:T(8,128)} %param.21, f32[8,32,1024]{2,1,0:T(8,128)S(1)} %reshape.195, pred[]{:T(512)S(6)} %eq.33, ...), kind=kLoop, calls=%fused_computation.46 | loop fusion | flops 1572864 | bytes 5505025 | tf_op jit(solution)/shard_map/scatter-add | solution.py:116
  82.3 4.1 %copy.73 = f32[1,16,32,1024]{3,2,1,0:T(8,128)} copy(f32[1,16,32,1024]{3,1,2,0:T(8,128)} %bitcast_dynamic-update-slice_fusion) | data formatting | bytes 4194304
  86.4 0.4 fusion.18
  86.8 0.2 reshape.200
  87.0 0.6 copy-done.1
  87.7 0.7 fusion.32
  88.4 1.6 %copy.74 = f32[1,8,32,1024]{3,2,1,0:T(8,128)} copy(f32[1,8,32,1024]{3,1,2,0:T(8,128)S(1)} %fusion.32) | data formatting | bytes 2097152
  (44 shorter events, 1.0 us)
Async XLA Ops:
  0.6 42.5 %copy-start = (f32[1,16,16]{2,1,0:T(8,128)S(1)}, f32[1,16,16]{2,1,0:T(8,128)}, u32[]{:S(2)}) copy-start(f32[1,16,16]{2,1,0:T(8,128)} %param.19) | copy-start | bytes 3076
  0.6 10.0 %copy-start.4 = (s32[16,1,4]{0,2,1:T(4,128)S(1)}, s32[16,1,4]{0,2,1:T(4,128)}, u32[]{:S(2)}) copy-start(s32[16,1,4]{0,2,1:T(4,128)} %param.22) | copy-start | bytes 772
  3.5 16.8 %copy-start.2 = (s32[1,32,1024]{2,1,0:T(8,128)S(1)}, s32[1,32,1024]{2,1,0:T(8,128)}, u32[]{:S(2)}) copy-start(s32[1,32,1024]{2,1,0:T(8,128)} %param.20) | copy-start | bytes 393220
  4.2 16.2 %copy-start.5 = (s32[16,1,4]{0,2,1:T(4,128)S(1)}, s32[16,1,4]{0,2,1:T(4,128)}, u32[]{:S(2)}) copy-start(s32[16,1,4]{0,2,1:T(4,128)} %param.26) | copy-start | bytes 772
  4.2 23.2 %collective-permute-start.1 = (f32[16,2,1024]{2,0,1:T(8,128)}, f32[16,2,1024]{2,0,1:T(8,128)}, u32[]{:S(2)}, u32[]{:S(2)}) collective-permute-start(f32[16,2,1024]{2,0,1:T(8,128)} %get-tuple-element.34), channel_id=1, source_target_pairs={{1,0},{2,1},{3,2},{4,3},{5,4},{6,5},{7,6},{8,7},{9,8},{10,9},{11,1... | collective-permute-start | bytes 393224 | tf_op jit(solution)/shard_map/ppermute | solution.py:26
  5.6 21.8 %collective-permute-start = (f32[16,2,1024]{2,0,1:T(8,128)}, f32[16,2,1024]{2,0,1:T(8,128)}, u32[]{:S(2)}, u32[]{:S(2)}) collective-permute-start(f32[16,2,1024]{2,0,1:T(8,128)} %get-tuple-element.33), channel_id=1, source_target_pairs={{0,1},{1,2},{2,3},{3,4},{4,5},{5,6},{6,7},{7,8},{8,9},{9,10},{10,1... | collective-permute-start | bytes 393224 | tf_op jit(solution)/shard_map/ppermute | solution.py:25
  11.1 12.1 %copy-start.6 = (s32[1,16,4]{1,2,0:T(4,128)S(1)}, s32[1,16,4]{1,2,0:T(4,128)}, u32[]{:S(2)}) copy-start(s32[1,16,4]{1,2,0:T(4,128)} %param.23) | copy-start | bytes 772
  11.4 11.9 %copy-start.9 = (s32[1,16]{1,0:T(1,128)S(1)}, s32[1,16]{1,0:T(1,128)}, u32[]{:S(2)}) copy-start(s32[1,16]{1,0:T(1,128)} %param.24) | copy-start | bytes 196
  12.9 22.6 %all-to-all-start = ((bf16[8,16,4,128]{3,0,2,1:T(8,128)(2,1)}), bf16[8,16,4,128]{3,0,2,1:T(8,128)(2,1)S(1)}, u32[]{:S(2)}, u32[]{:S(2)}) async-start(bf16[8,16,4,128]{3,0,2,1:T(8,128)(2,1)} %bitcast.9), calls=%async_computation | async-start | bytes 262144 | tf_op jit(solution)/shard_map/all_to_all | solution.py:90
  20.3 5.3 %copy-start.10 = (s32[16,1]{0,1:T(1,128)S(1)}, s32[16,1]{0,1:T(1,128)}, u32[]{:S(2)}) copy-start(s32[16,1]{0,1:T(1,128)} %param.28) | copy-start | bytes 196
  28.6 1.1 %copy-start.8 = (f32[1,16]{1,0:T(1,128)S(1)}, f32[1,16]{1,0:T(1,128)}, u32[]{:S(2)}) copy-start(f32[1,16]{1,0:T(1,128)} %param.18) | copy-start | bytes 196
  35.5 27.3 %all-to-all-start.2 = ((bf16[1,16,4,128]{3,2,0,1:T(4,128)(2,1)}), bf16[1,16,4,128]{3,2,0,1:T(4,128)(2,1)}, u32[]{:S(2)}, u32[]{:S(2)}) async-start(bf16[1,16,4,128]{3,2,0,1:T(4,128)(2,1)} %fusion.41), calls=%async_computation.2 | async-start | bytes 32768 | tf_op jit(solution)/shard_map/all_to_all | solution.py:126
  41.5 5.9 %collective-permute-start.2 = (bf16[8,16,4,128]{3,0,2,1:T(8,128)(2,1)S(1)}, bf16[8,16,4,128]{3,0,2,1:T(8,128)(2,1)S(1)}, u32[]{:S(2)}, u32[]{:S(2)}) collective-permute-start(bf16[8,16,4,128]{3,0,2,1:T(8,128)(2,1)S(1)} %all-to-all-done), channel_id=1, source_target_pairs={{0,16},{16,0},{1,17},{17,1},{2,18},{18,2},{3,19},{19,3},{4,20},{20... | collective-permute-start | bytes 393224 | tf_op jit(solution)/shard_map/ppermute | solution.py:15
  59.8 10.1 %copy-start.7 = (s32[1,16,4]{1,2,0:T(4,128)S(1)}, s32[1,16,4]{1,2,0:T(4,128)}, u32[]{:S(2)}) copy-start(s32[1,16,4]{1,2,0:T(4,128)} %param.27) | copy-start | bytes 772
  62.7 14.0 %all-to-all-start.1 = ((bf16[8,16,4,128]{3,0,2,1:T(8,128)(2,1)}), bf16[8,16,4,128]{3,0,2,1:T(8,128)(2,1)}, u32[]{:S(2)}, u32[]{:S(2)}) async-start(bf16[8,16,4,128]{3,0,2,1:T(8,128)(2,1)} %fusion.29), calls=%async_computation.1 | async-start | bytes 262144 | tf_op jit(solution)/shard_map/all_to_all | solution.py:123
  68.7 4.0 %collective-permute-start.4 = (bf16[1,16,4,128]{3,2,0,1:T(4,128)(2,1)}, bf16[1,16,4,128]{3,2,0,1:T(4,128)(2,1)S(1)}, u32[]{:S(2)}, u32[]{:S(2)}) collective-permute-start(bf16[1,16,4,128]{3,2,0,1:T(4,128)(2,1)} %all-to-all-done.2), channel_id=1, source_target_pairs={{0,16},{16,0},{1,17},{17,1},{2,18},{18,2},{3,19},{19,3},{4,20},{20... | collective-permute-start | bytes 49160 | tf_op jit(solution)/shard_map/ppermute | solution.py:15
  72.8 0.6 copy-start.3
  76.7 9.7 %collective-permute-start.3 = (bf16[8,16,4,128]{3,0,2,1:T(8,128)(2,1)}, bf16[8,16,4,128]{3,0,2,1:T(8,128)(2,1)S(1)}, u32[]{:S(2)}, u32[]{:S(2)}) collective-permute-start(bf16[8,16,4,128]{3,0,2,1:T(8,128)(2,1)} %all-to-all-done.1), channel_id=1, source_target_pairs={{0,16},{16,0},{1,17},{17,1},{2,18},{18,2},{3,19},{19,3},{4,20},{20... | collective-permute-start | bytes 393224 | tf_op jit(solution)/shard_map/ppermute | solution.py:15
  86.4 1.2 %copy-start.1 = (f32[8,32,1024]{2,0,1:T(8,128)S(1)}, f32[8,32,1024]{2,0,1:T(8,128)}, u32[]{:S(2)}) copy-start(f32[8,32,1024]{2,0,1:T(8,128)} %get-tuple-element.24) | copy-start | bytes 3145732
where the time goes:
time: 90.8 us; the launch traced here: 89.9 us
  starting transfers between devices  28.5 us (31%)
  other arithmetic  23.2 us (26%)
  local copies, waits for them, and re-layouts  20.7 us (23%)
  matrix products  12.9 us (14%)
  waiting for transfers between devices  3.66 us (4%)
  between operations  1.01 us (1%)
    unnamed x30, local copies, waits for them, and re-layouts  11.5 us
    all_to_all x1, starting transfers between devices, per_device(): lax.all_to_all(picked, 'tile', split_axis=1, concat_axis=1, tiled=True)  7.4 us
    all_to_all x1, starting transfers between devices, per_device(): lax.all_to_all(column.astype(jnp.bfloat16), 'tile', split_axis=1, concat_...  6.07 us
    all_to_all x1, starting transfers between devices, per_device(): lax.all_to_all(contrib.astype(jnp.bfloat16), 'tile', split_axis=1, concat...  5.99 us
    dot_general x2, matrix products, weigh_blocks(): jnp.einsum('fsck,sckm->fscm', picked, weights, preferred_element_type=jnp...  5.15 us
    mul x2, other arithmetic, per_device(): widened = (widened + rates * (beside_all - 4.0 * widened)) * inside  4.58 us
    convert_element_type x1, other arithmetic, per_device(): flux_blocks16 = flux_local.astype(jnp.bfloat16).reshape(NF, nblocks, BLK)  4.51 us
    scatter-add x1, other arithmetic, per_device(): new_state = new_state.at[:NF].add(surface)  4.47 us
  transfers between devices with their start and end apart: 8, of which 2 were waited for; matrix products, arithmetic and copies ran while one was open for 55% of the time, Pallas kernels for 0%

commit v1 on v0

v1 whole, which is shorter than its diff:
```python
import functools

import jax
import jax.numpy as jnp
from jax import lax
from jax.experimental import pallas as pl
from jax.experimental.pallas import tpu as pltpu
from jax.sharding import PartitionSpec as P

NF = 8
BLK = 128
CAP = 4
NSUB = 2
SUB = 8
F32 = jnp.float32
BF16 = jnp.bfloat16
VMEM_LIMIT = 40 * 1024 * 1024


def tile_view(grid):
    levels, rows, cells = grid.shape
    split = grid.reshape(levels, rows // SUB, SUB, cells // BLK, BLK)
    return split.transpose(0, 1, 3, 2, 4).reshape(levels * rows * cells // BLK, BLK)


def from_tile_view(tiles, levels, rows, cells):
    split = tiles.reshape(levels, rows // SUB, cells // BLK, SUB, BLK)
    return split.transpose(0, 1, 3, 2, 4).reshape(levels, rows, cells)


def tile_row(row, x, columns):
    return (lax.div(row, SUB) * columns + x) * SUB + lax.rem(row, SUB)


def block_tile_row(block, columns):
    return tile_row(lax.div(block, columns), lax.rem(block, columns), columns)


def aligned(index, step):
    return pl.multiple_of(index * step, step)


def loop(count, body, unroll=1):
    def step(i, carry):
        body(i)
        return carry

    lax.fori_loop(0, count, step, 0, unroll=unroll)


def pick_kernel(dims, src, state, sent, slab_a, slab_b):
    rows, columns, levels, tiles = dims
    comp, tile = lax.axis_index("comp"), lax.axis_index("tile")
    level_stride = rows * columns
    other = (1 - comp) * tiles

    def one_tile(t):
        for pair in range(CAP // 2):
            two = []
            for k in (2 * pair, 2 * pair + 1):
                start = block_tile_row(src[t, k], columns)
                two.append(state[pl.ds(start, NF, stride=level_stride), :])
            both = jnp.concatenate(two, axis=0).astype(BF16)
            sent[other + t, pl.ds(2 * NF * pair, 2 * NF), :] = both
        sent[comp * tiles + t] = jnp.zeros((CAP * NF, BLK), BF16)

    loop(tiles, one_tile, unroll=4)
    even = lax.rem(tile, 2) == 0
    for slab, first in (
        (slab_a, jnp.where(even, rows - NSUB, 0)),
        (slab_b, jnp.where(even, 0, rows - NSUB)),
    ):
        for i in range(NSUB):
            for x in range(columns):
                start = tile_row(first + i, x, columns)
                value = state[pl.ds(start, levels, stride=level_stride), :]
                slab[(i * columns + x) * levels : (i * columns + x + 1) * levels, :] = value


def prepare_kernel(dims, count, state, lagged, weight, blocks, lagged_blocks, column_sums):
    rows, columns, levels, tiles = dims
    level_stride = rows * columns
    comp = lax.axis_index("comp")
    atmosphere = jnp.where(comp == 0, 1.0, 0.0).astype(F32)

    def one_row(r):
        for x in range(columns):
            start = tile_row(r, x, columns)
            block = r * columns + x
            blocks[pl.ds(aligned(block, levels), levels), :] = state[
                pl.ds(start, levels, stride=level_stride), :
            ]
            lagged_blocks[pl.ds(aligned(block, NF), NF), :] = (
                lagged[pl.ds(start, NF, stride=level_stride), :] * atmosphere
            )

    loop(rows, one_row, unroll=2)
    ones = jnp.ones((2 * SUB, BLK), BF16)

    def one_tile(t):
        live = count[t]
        rows_of = lax.broadcasted_iota(jnp.int32, (SUB, BLK), 0)
        sums = jnp.zeros((SUB, BLK), F32)
        for k in range(CAP):
            column = jnp.dot(ones, weight[t, k], preferred_element_type=F32)[:SUB]
            column = column * jnp.where(k < live, 1.0, 0.0).astype(F32)
            sums = jnp.where((rows_of == k) | (rows_of == k + CAP), column, sums)
        high = sums.astype(BF16).astype(F32)
        column_sums[t] = jnp.where(rows_of < CAP, high, sums - high)

    loop(tiles, one_tile, unroll=4)


def diffuse_kernel(dims, blocks, from_a, from_b, kappa, col_mix, mask, base, deep, stepped):
    rows, columns, levels, tiles = dims
    tile = lax.axis_index("tile")
    even = lax.rem(tile, 2) == 0
    above_in = jnp.where(tile > 0, 1.0, 0.0).astype(F32)
    below_in = jnp.where(tile < tiles - 1, 1.0, 0.0).astype(F32)
    rate = kappa[...]
    keep = 1.0 - 4.0 * rate
    lane = lax.broadcasted_iota(jnp.int32, (levels, BLK), 1)

    def load_row(ref, r):
        return [
            ref[pl.ds(aligned(r * columns + x, levels), levels), :] for x in range(columns)
        ]

    def slab_row(above, i):
        first, second = (from_b, from_a) if above else (from_a, from_b)
        return [
            jnp.where(even, p, q)
            for p, q in zip(load_row(first, i), load_row(second, i), strict=True)
        ]

    def stencil(up, mid, down):
        right_roll = [pltpu.roll(v, 1, 1) for v in mid]
        left_roll = [pltpu.roll(v, BLK - 1, 1) for v in mid]
        out = []
        for x in range(columns):
            west = jnp.where(lane == 0, right_roll[x - 1], right_roll[x])
            east = jnp.where(lane == BLK - 1, left_roll[(x + 1) % columns], left_roll[x])
            out.append(keep * mid[x] + rate * (up[x] + down[x] + (west + east)))
        return out

    def store_stepped(r, values, scale=None):
        for x, v in enumerate(values):
            v = v if scale is None else v * scale
            stepped[pl.ds(aligned((r + 1) * columns + x, levels), levels), :] = v

    above = [slab_row(True, i) for i in range(NSUB)]
    store_stepped(-1, stencil(above[0], above[1], load_row(blocks, 0)), above_in)
    store_stepped(0, stencil(above[1], load_row(blocks, 0), load_row(blocks, 1)))
    below = [slab_row(False, i) for i in range(NSUB)]
    store_stepped(
        rows - 1, stencil(load_row(blocks, rows - 2), load_row(blocks, rows - 1), below[0])
    )
    store_stepped(rows, stencil(load_row(blocks, rows - 1), below[0], below[1]), below_in)

    def first_step(i):
        r = i + 1
        store_stepped(
            r, stencil(load_row(blocks, r - 1), load_row(blocks, r), load_row(blocks, r + 1))
        )

    loop(rows - 2, first_step)
    mix = col_mix[...]
    mix_high = mix.astype(BF16)
    mix_low = (mix - mix_high.astype(F32)).astype(BF16)

    def second_step(r):
        done = stencil(load_row(stepped, r), load_row(stepped, r + 1), load_row(stepped, r + 2))
        whole = jnp.concatenate(done, axis=1)
        high = whole.astype(BF16)
        low = (whole - high.astype(F32)).astype(BF16)
        mixed = (
            jnp.dot(mix_high, high, preferred_element_type=F32)
            + jnp.dot(mix_high, low, preferred_element_type=F32)
            + jnp.dot(mix_low, high, preferred_element_type=F32)
        )
        moved = whole + 0.5 * jnp.tanh(mixed)
        land = mask[0, pl.ds(r, 1), :].astype(F32)
        top = moved[:NF] - (0.5 * (1.0 - land)) * whole[:NF]
        rest = moved[NF:]
        for x in range(columns):
            where = r * columns + x
            cells = slice(x * BLK, (x + 1) * BLK)
            base[pl.ds(aligned(where, NF), NF), :] = top[:, cells]
            deep[pl.ds(aligned(where, levels - NF), levels - NF), :] = rest[:, cells]

    loop(rows, second_step)


def surface_kernel(
    dims, dst, live_in, src, live_out, arrived, weight_in, base, lagged, mask, weight_out, column_sums,
    sent, top, flux, numerator, denominator,
):
    rows, columns, _, tiles = dims
    comp = lax.axis_index("comp")
    other = (1 - comp) * tiles

    def clear(r):
        for x in range(columns):
            where = pl.ds(aligned(r * columns + x, NF), NF)
            numerator[where, :] = jnp.zeros((NF, BLK), F32)
            denominator[where, :] = jnp.zeros((NF, BLK), F32)

    loop(rows, clear, unroll=4)
    ones = jnp.ones((NF, BLK), F32)

    def receive(t):
        got = arrived[other + t].astype(F32)
        for k in range(CAP):
            both = jnp.concatenate([got[k * NF : (k + 1) * NF], ones], axis=0).astype(BF16)
            product = jnp.dot(both, weight_in[t, k], preferred_element_type=F32)
            live = jnp.where(k < live_in[t], 1.0, 0.0).astype(F32)
            product = product * live
            where = pl.ds(aligned(dst[t, k], NF), NF)
            numerator[where, :] += product[:NF]
            denominator[where, :] += product[NF:]

    loop(tiles, receive, unroll=4)

    def one_row(r):
        land_row = mask[0, pl.ds(r, 1), :].astype(F32)
        for x in range(columns):
            where = pl.ds(aligned(r * columns + x, NF), NF)
            land = land_row[:, x * BLK : (x + 1) * BLK]
            received = numerator[where, :] / jnp.maximum(denominator[where, :], 1.0)
            incoming = lagged[where, :] + received
            state = base[where, :] + land * incoming
            top[where, :] = state
            flux[where, :] = land * jnp.tanh(state - incoming)

    loop(rows, one_row)

    def send(t):
        for pair in range(CAP // 2):
            two = []
            for k in (2 * pair, 2 * pair + 1):
                picked = flux[pl.ds(aligned(src[t, k], NF), NF), :].astype(BF16)
                product = jnp.dot(picked, weight_out[t, k], preferred_element_type=F32)
                two.append(product * jnp.where(k < live_out[t], 1.0, 0.0).astype(F32))
            both = jnp.concatenate(two, axis=0).astype(BF16)
            sent[other + t, pl.ds(2 * NF * pair, 2 * NF), :] = both
        sums = jnp.concatenate([column_sums[t], jnp.zeros((SUB, BLK), F32)], axis=0)
        sent[comp * tiles + t, pl.ds(0, 2 * SUB), :] = sums.astype(BF16)
        sent[comp * tiles + t, pl.ds(2 * SUB, 2 * SUB), :] = jnp.zeros((2 * SUB, BLK), BF16)

    loop(tiles, send, unroll=4)


def write_kernel(dims, top, deep, flux, new_state, land_flux):
    rows, columns, levels, _ = dims
    comp = lax.axis_index("comp")
    on_land = jnp.where(comp == 1, 1.0, 0.0).astype(F32)
    depth = levels - NF

    def one(rt):
        for x in range(columns):
            for level in range(NF):
                out = pl.ds(aligned((level * (rows // SUB) + rt) * columns + x, SUB), SUB)
                start = (rt * SUB * columns + x) * NF + level
                new_state[out, :] = top[pl.ds(start, SUB, stride=columns * NF), :]
                land_flux[out, :] = flux[pl.ds(start, SUB, stride=columns * NF), :] * on_land
            for level in range(depth):
                out = pl.ds(aligned(((level + NF) * (rows // SUB) + rt) * columns + x, SUB), SUB)
                start = (rt * SUB * columns + x) * depth + level
                new_state[out, :] = deep[pl.ds(start, SUB, stride=columns * depth), :]

    loop(rows // SUB, one)


def return_kernel(dims, dst, arrived, land_flux, fluxes, numerator, denominator):
    rows, columns, _, tiles = dims
    comp = lax.axis_index("comp")
    other = (1 - comp) * tiles
    level_stride = rows * columns

    def clear(t):
        for k in range(CAP):
            where = pl.ds(aligned(dst[t, k], NF), NF)
            numerator[where, :] = jnp.zeros((NF, BLK), F32)
            denominator[where, :] = jnp.zeros((NF, BLK), F32)

    loop(tiles, clear, unroll=4)

    def copy(i):
        where = pl.ds(aligned(i, columns * SUB), columns * SUB)
        fluxes[where, :] = land_flux[where, :]

    loop(NF * rows // SUB, copy, unroll=4)

    def receive(t):
        got = arrived[other + t].astype(F32)
        sums = arrived[comp * tiles + t].astype(F32)
        sums = sums[:CAP] + sums[CAP : 2 * CAP]
        for k in range(CAP):
            where = pl.ds(aligned(dst[t, k], NF), NF)
            numerator[where, :] += got[k * NF : (k + 1) * NF]
            denominator[where, :] += jnp.broadcast_to(sums[k : k + 1], (NF, BLK))

    loop(tiles, receive, unroll=4)

    def finish(t):
        for k in range(CAP):
            block = dst[t, k]
            where = pl.ds(aligned(block, NF), NF)
            out = pl.ds(block_tile_row(block, columns), NF, stride=level_stride)
            value = numerator[where, :] / jnp.maximum(denominator[where, :], 1.0)
            fluxes[out, :] = land_flux[out, :] + value

    loop(tiles, finish, unroll=4)


def call(kernel, scalars, arrays, outs, scratch=(), cost=0):
    smem = pl.BlockSpec(memory_space=pltpu.SMEM)
    vmem = pl.BlockSpec(memory_space=pltpu.VMEM)
    return pl.pallas_call(
        kernel,
        out_shape=outs,
        in_specs=[smem] * len(scalars) + [vmem] * len(arrays),
        out_specs=tuple([vmem] * len(outs)),
        scratch_shapes=list(scratch),
        compiler_params=pltpu.CompilerParams(vmem_limit_bytes=VMEM_LIMIT),
        cost_estimate=pl.CostEstimate(flops=cost, bytes_accessed=cost // 4, transcendentals=0),
    )(*scalars, *arrays)


def per_device(
    state,
    kappa,
    col_mix,
    surface_mask,
    lagged_flux,
    a2l_src,
    a2l_dst,
    a2l_count,
    a2l_weight,
    l2a_src,
    l2a_dst,
    l2a_count,
    l2a_weight,
):
    fields = state[0]
    levels, rows, cells = fields.shape
    columns = cells // BLK
    nblocks = rows * columns
    tiles = lax.axis_size("tile")
    dims = (rows, columns, levels, tiles)
    shape = jax.ShapeDtypeStruct
    kernel = lambda f: functools.partial(f, dims)
    state_tiles = tile_view(fields)
    slab = shape((NSUB * columns * levels, BLK), F32)
    parcel = shape((2 * tiles, CAP * NF, BLK), BF16)
    sent, slab_a, slab_b = call(
        kernel(pick_kernel), [a2l_src[:, 0, :]], [state_tiles], [parcel, slab, slab],
        cost=4_000_000,
    )
    arrived = lax.all_to_all(sent, ("comp", "tile"), split_axis=0, concat_axis=0, tiled=True)
    from_a = lax.ppermute(slab_a, "tile", [(i, i ^ 1) for i in range(tiles)])
    pairs = [(i, i + 1) for i in range(1, tiles - 1, 2)]
    from_b = lax.ppermute(slab_b, "tile", pairs + [(j, i) for i, j in pairs])
    blocks, lagged_blocks, column_sums = call(
        kernel(prepare_kernel), [l2a_count[:, 0]],
        [state_tiles, tile_view(lagged_flux), l2a_weight[:, 0]],
        [pltpu.VMEM((nblocks * levels, BLK), F32), pltpu.VMEM((nblocks * NF, BLK), F32),
         pltpu.VMEM((tiles, SUB, BLK), F32)],
        cost=20_000_000,
    )
    base, deep = call(
        kernel(diffuse_kernel), [],
        [blocks, from_a, from_b, jnp.broadcast_to(kappa[0][:, None], (levels, BLK)), col_mix[0],
         surface_mask],
        [pltpu.VMEM((nblocks * NF, BLK), F32), pltpu.VMEM((nblocks * (levels - NF), BLK), F32)],
        scratch=[pltpu.VMEM(((rows + 2) * columns * levels, BLK), F32)],
        cost=40_000_000,
    )
    sent_back, top, flux = call(
        kernel(surface_kernel), [a2l_dst[0], a2l_count[0], l2a_src[:, 0, :], l2a_count[:, 0]],
        [arrived, a2l_weight[0], base, lagged_blocks, surface_mask, l2a_weight[:, 0], column_sums],
        [parcel, pltpu.VMEM((nblocks * NF, BLK), F32), pltpu.VMEM((nblocks * NF, BLK), F32)],
        scratch=[pltpu.VMEM((nblocks * NF, BLK), F32), pltpu.VMEM((nblocks * NF, BLK), F32)],
        cost=20_000_000,
    )
    returned = lax.all_to_all(sent_back, ("comp", "tile"), split_axis=0, concat_axis=0, tiled=True)
    new_state, land_flux = call(
        kernel(write_kernel), [], [top, deep, flux],
        [shape((levels * nblocks, BLK), F32), pltpu.VMEM((NF * nblocks, BLK), F32)],
        cost=20_000_000,
    )
    (fluxes,) = call(
        kernel(return_kernel), [l2a_dst[0]], [returned, land_flux],
        [shape((NF * nblocks, BLK), F32)],
        scratch=[pltpu.VMEM((nblocks * NF, BLK), F32), pltpu.VMEM((nblocks * NF, BLK), F32)],
        cost=10_000_000,
    )
    return (
        from_tile_view(new_state, levels, rows, cells)[None],
        from_tile_view(fluxes, NF, rows, cells)[None],
    )


def solution(mesh):
    return jax.shard_map(
        per_device,
        mesh=mesh,
        in_specs=(
            P("comp", None, "tile", None),
            P("comp", None),
            P("comp", None, None),
            P("comp", "tile", None),
            P(None, "tile", None),
            P(None, "tile", None),
            P("tile", None, None),
            P("tile", None),
            P("tile", None, None, None, None),
            P(None, "tile", None),
            P("tile", None, None),
            P(None, "tile"),
            P(None, "tile", None, None, None),
        ),
        out_specs=(P("comp", None, "tile", None), P("comp", None, "tile", None)),
        check_vma=False,
    )
```

time: 90.8 us -> 70 us (0.77)
  Pallas kernels: 0 us -> 28.2 us
  other arithmetic: 23.2 us -> 0 us
  matrix products: 12.9 us -> 0 us
  starting transfers between devices: 28.5 us -> 15.8 us
    pallas_call x0 -> x6, Pallas kernels: none -> 28.2 us  [call(): pl.pallas_call(kernel, out_shape=outs, in_specs=[smem] * len(scalars) + [...]
    dot_general x7 -> x0, matrix products: 12.9 us -> none  [the longest x2 5.15 us: weigh_blocks(): jnp.einsum('fsck,sckm->fscm', picked, weights, preferred_element_type=jnp...]
    unnamed x30 -> x50, local copies, waits for them, and re-layouts: 11.5 us -> 18.9 us
    ppermute x5 -> x2, starting transfers between devices: 8.99 us -> 1.62 us  [the longest x1 1.3 us: per_device(): from_b = lax.ppermute(slab_b, 'tile', pairs + [(j, i) for i, j in pairs])]
    convert_element_type x5 -> x0, other arithmetic: 5.35 us -> none  [the longest x1 4.51 us: per_device(): flux_blocks16 = flux_local.astype(jnp.bfloat16).reshape(NF, nblocks, BLK)]
    all_to_all x3 -> x2, starting transfers between devices: 19.5 us -> 14.2 us  [the longest x1 7.33 us: per_device(): lax.all_to_all(sent, ('comp', 'tile'), split_axis=0, concat_axis=0, tiled...]
    mul x4 -> x0, other arithmetic: 4.61 us -> none  [the longest x2 4.58 us: per_device(): widened = (widened + rates * (beside_all - 4.0 * widened)) * inside]
    scatter-add x1 -> x0, other arithmetic: 4.47 us -> none  [per_device(): new_state = new_state.at[:NF].add(surface)]
  transfers between devices with their start and end apart: 8 -> 4, of which waited for: 2 -> 1; matrix products, arithmetic and copies ran while one was open for 55% -> 1% of each run, Pallas kernels for 0% -> 28%
where the time goes in v1:
time: 70 us; the launch traced here: 69.3 us
  Pallas kernels  28.2 us (40%)
  local copies, waits for them, and re-layouts  20.7 us (30%)
  starting transfers between devices  15.8 us (23%)
  waiting for transfers between devices  3.92 us (6%)
  between operations  0.72 us (1%)
    pallas_call x6, Pallas kernels, call(): pl.pallas_call(kernel, out_shape=outs, in_specs=[smem] * len(scalars) + [...  28.2 us
    unnamed x50, local copies, waits for them, and re-layouts  18.9 us
    all_to_all x1, starting transfers between devices, per_device(): lax.all_to_all(sent, ('comp', 'tile'), split_axis=0, concat_axis=0, tiled...  7.33 us
    all_to_all x1, starting transfers between devices, per_device(): lax.all_to_all(sent_back, ('comp', 'tile'), split_axis=0, concat_axis=0,...  6.84 us
    all_to_all x1, waiting for transfers between devices, per_device(): lax.all_to_all(sent_back, ('comp', 'tile'), split_axis=0, concat_axis=0,...  3.92 us
  transfers between devices with their start and end apart: 4, of which 1 were waited for; matrix products, arithmetic and copies ran while one was open for 1% of the time, Pallas kernels for 28%

profile of v1, /device:TPU:0, one launch (start us, length us, event | category | flops | bytes accessed | tf_op | source)
XLA Modules:
  0.0 69.3 jit_solution(6704589862047829049)
XLA Ops:
  0.6 0.0 copy-start.22
  0.6 0.0 copy-start.23
  0.7 0.8 %copy.15.src = s32[16,4]{1,0:T(8,128)S(1)} copy(s32[16,4]{0,1:T(4,128)} %bitcast.41) | data formatting | bytes 512 | tf_op jit(solution)/shard_map/squeeze | solution.py:357
  1.4 0.0 copy-start
  1.4 1.6 %copy-done = f32[1,16,32,1024]{3,2,1,0:T(8,128)S(1)} copy-done((f32[1,16,32,1024]{3,2,1,0:T(8,128)S(1)}, f32[1,16,32,1024]{3,2,1,0:T(8,128)}, u32[]{:S(2)}) %copy-start) | copy-done | bytes 2097176
  3.0 2.2 %shard_map.140 = (bf16[32,32,128]{2,1,0:T(8,128)(2,1)}, f32[256,128]{1,0:T(8,128)}, f32[256,128]{1,0:T(8,128)}) custom-call(s32[16,4]{1,0:T(8,128)S(1)} %copy.15.src, f32[4096,128]{1,0:T(8,128)S(1)} %bitcast.30), custom_call_target="tpu_custom_call" | custom-call | flops 4000000 | bytes 1000000 | tf_op jit(solution)/shard_map/pallas_call | solution.py:319
  5.2 7.3 %all-to-all-start = ((bf16[32,32,128]{2,1,0:T(8,128)(2,1)}), bf16[32,32,128]{2,1,0:T(8,128)(2,1)S(1)}, u32[]{:S(2)}, u32[]{:S(2)}) async-start(bf16[32,32,128]{2,1,0:T(8,128)(2,1)} %get-tuple-element.15), calls=%async_computation | async-start | bytes 524288 | tf_op jit(solution)/shard_map/all_to_all | solution.py:360
  12.6 0.3 collective-permute-start
  12.9 1.3 %collective-permute-start.1 = (f32[256,128]{1,0:T(8,128)}, f32[256,128]{1,0:T(8,128)}, u32[]{:S(2)}, u32[]{:S(2)}) collective-permute-start(f32[256,128]{1,0:T(8,128)} %get-tuple-element.18), channel_id=1, source_target_pairs={{1,2},{3,4},{5,6},{7,8},{9,10},{11,12},{13,14},{2,1},{4,3},{6,5},{... | collective-permute-start | bytes 393224 | tf_op jit(solution)/shard_map/ppermute | solution.py:363
  14.2 0.0 copy-done.22
  14.2 0.1 copy.16.dst
  14.3 0.0 copy-done.23
  14.3 0.1 copy.17.src
  14.3 0.0 copy-done.1
  14.3 1.6 %copy-done.2 = bf16[16,1,4,128,128]{4,3,2,1,0:T(8,128)(2,1)S(1)} copy-done((bf16[16,1,4,128,128]{4,3,2,1,0:T(8,128)(2,1)S(1)}, bf16[16,1,4,128,128]{4,3,2,1,0:T(8,128)(2,1)}, u32[]{:S(2)}) %copy-start.2) | copy-done | bytes 2097176
  15.9 1.2 %copy-done.9 = f32[8,32,1024]{2,1,0:T(8,128)S(1)} copy-done((f32[8,32,1024]{2,1,0:T(8,128)S(1)}, f32[8,32,1024]{2,1,0:T(8,128)}, u32[]{:S(2)}) %copy-start.9) | copy-done | bytes 1048600
  17.2 0.7 copy-done.19
  17.8 3.5 %shard_map.141 = (f32[4096,128]{1,0:T(8,128)S(1)}, f32[2048,128]{1,0:T(8,128)S(1)}, f32[16,8,128]{2,1,0:T(8,128)S(1)}) custom-call(s32[16]{0:T(128)S(1)} %bitcast.37, f32[4096,128]{1,0:T(8,128)S(1)} %bitcast.31, f32[2048,128]{1,0:T(8,128)S(1)} %bitcast.35, bf16[16,4,128,128]{3,2,1,0:T(8,128)(2,1)S(1)} %bitcast.32), custom_call_target="tpu_custom_call" | custom-call | flops 20000000 | bytes 5000000 | tf_op jit(solution)/shard_map/pallas_call | solution.py:319
  21.3 1.0 %copy-done.10 = f32[2048,128]{1,0:T(8,128)} copy-done((f32[2048,128]{1,0:T(8,128)}, f32[2048,128]{1,0:T(8,128)S(1)}, u32[]{:S(2)}) %copy-start.10) | copy-done | bytes 1048600
  22.3 0.6 copy-done.16
  22.9 0.0 collective-permute-done.from_a
  22.9 0.0 collective-permute-done.1.from_b
  23.0 0.0 copy-done.24
  23.0 0.1 broadcast_in_dim.8.kappa
  23.0 0.0 copy-done.14
  23.0 0.0 copy-done.18
  23.0 12.6 %shard_map.142 = (f32[2048,128]{1,0:T(8,128)S(1)}, f32[2048,128]{1,0:T(8,128)S(1)}) custom-call(f32[4096,128]{1,0:T(8,128)S(1)} %get-tuple-element.16.blocks, f32[256,128]{1,0:T(8,128)} %collective-permute-done.from_a, f32[256,128]{1,0:T(8,128)} %collective-permute-done.1.from_b, f32[16,128]{1,0:T(8,128)S(1)} %broadcast_in_dim.8.kappa, ...), custom_call_target="tpu_custom_call" | custom-call | flops 40000000 | bytes 10000000 | tf_op jit(solution)/shard_map/pallas_call | solution.py:319
  35.6 0.0 copy-start.12
  35.7 1.0 %copy-done.12 = f32[2048,128]{1,0:T(8,128)} copy-done((f32[2048,128]{1,0:T(8,128)}, f32[2048,128]{1,0:T(8,128)S(1)}, u32[]{:S(2)}) %copy-start.12) | copy-done | bytes 1048600
  36.6 0.0 all-to-all-done.arrived
  36.6 0.0 copy-done.3
  36.6 1.6 %copy-done.4 = bf16[1,16,4,128,128]{4,3,2,1,0:T(8,128)(2,1)S(1)} copy-done((bf16[1,16,4,128,128]{4,3,2,1,0:T(8,128)(2,1)S(1)}, bf16[1,16,4,128,128]{4,3,2,1,0:T(8,128)(2,1)}, u32[]{:S(2)}) %copy-start.4) | copy-done | bytes 2097176
  38.2 1.2 %copy-done.11 = f32[2048,128]{1,0:T(8,128)S(1)} copy-done((f32[2048,128]{1,0:T(8,128)S(1)}, f32[2048,128]{1,0:T(8,128)}, u32[]{:S(2)}) %copy-start.11) | copy-done | bytes 1048600
  39.4 1.2 %copy-done.13 = f32[2048,128]{1,0:T(8,128)S(1)} copy-done((f32[2048,128]{1,0:T(8,128)S(1)}, f32[2048,128]{1,0:T(8,128)}, u32[]{:S(2)}) %copy-start.13) | copy-done | bytes 1048600
  40.7 0.8 %copy-done.17 = f32[16,8,128]{2,1,0:T(8,128)S(1)} copy-done((f32[16,8,128]{2,1,0:T(8,128)S(1)}, f32[16,8,128]{2,1,0:T(8,128)}, u32[]{:S(2)}) %copy-start.17) | copy-done | bytes 65560
  41.5 0.7 copy-done.20
  42.2 0.7 copy-done.21
  42.8 3.9 %shard_map.143 = (bf16[32,32,128]{2,1,0:T(8,128)(2,1)S(1)}, f32[2048,128]{1,0:T(8,128)S(1)}, f32[2048,128]{1,0:T(8,128)S(1)}) custom-call(s32[16,4]{1,0:T(8,128)S(1)} %copy.16.dst, s32[16]{0:T(128)S(1)} %bitcast.39, s32[16,4]{1,0:T(8,128)S(1)} %copy.17.src, s32[16]{0:T(128)S(1)} %bitcast.38, bf16[32,32,128]{2,1,0:T(8,128)(2,1)S(1)} %all-to-all-done.arrived, ...), custom_call_target="tpu_custom_call" | custom-call | flops 20000000 | bytes 5000000 | tf_op jit(solution)/shard_map/pallas_call | solution.py:319
  46.7 1.0 %copy-done.5 = f32[2048,128]{1,0:T(8,128)} copy-done((f32[2048,128]{1,0:T(8,128)}, f32[2048,128]{1,0:T(8,128)S(1)}, u32[]{:S(2)}) %copy-start.5) | copy-done | bytes 1048600
  47.7 1.0 %copy-done.7 = f32[2048,128]{1,0:T(8,128)} copy-done((f32[2048,128]{1,0:T(8,128)}, f32[2048,128]{1,0:T(8,128)S(1)}, u32[]{:S(2)}) %copy-start.7) | copy-done | bytes 1048600
  48.6 0.7 copy-done.15
  49.3 6.8 %all-to-all-start.1 = ((bf16[32,32,128]{2,1,0:T(8,128)(2,1)}), bf16[32,32,128]{2,1,0:T(8,128)(2,1)S(1)}, u32[]{:S(2)}, u32[]{:S(2)}) async-start(bf16[32,32,128]{2,1,0:T(8,128)(2,1)} %copy-done.15), calls=%async_computation.1 | async-start | bytes 524288 | tf_op jit(solution)/shard_map/all_to_all | solution.py:386
  56.2 0.8 %copy.18.dst = s32[16,4]{1,0:T(8,128)S(1)} copy(s32[16,4]{0,1:T(4,128)} %bitcast.44) | data formatting | bytes 512 | tf_op jit(solution)/shard_map/squeeze | solution.py:393
  56.9 1.2 %copy-done.6 = f32[2048,128]{1,0:T(8,128)S(1)} copy-done((f32[2048,128]{1,0:T(8,128)S(1)}, f32[2048,128]{1,0:T(8,128)}, u32[]{:S(2)}) %copy-start.6) | copy-done | bytes 1048600
  58.2 1.2 %copy-done.8 = f32[2048,128]{1,0:T(8,128)S(1)} copy-done((f32[2048,128]{1,0:T(8,128)S(1)}, f32[2048,128]{1,0:T(8,128)}, u32[]{:S(2)}) %copy-start.8) | copy-done | bytes 1048600
  59.4 3.1 %shard_map.144 = (f32[4096,128]{1,0:T(8,128)}, f32[2048,128]{1,0:T(8,128)S(1)}) custom-call(f32[2048,128]{1,0:T(8,128)S(1)} %copy-done.6, f32[2048,128]{1,0:T(8,128)S(1)} %get-tuple-element.23.deep, f32[2048,128]{1,0:T(8,128)S(1)} %copy-done.8), custom_call_target="tpu_custom_call" | custom-call | flops 20000000 | bytes 5000000 | tf_op jit(solution)/shard_map/pallas_call | solution.py:319
  62.5 3.9 %all-to-all-done.1.arrived = bf16[32,32,128]{2,1,0:T(8,128)(2,1)S(1)} async-done(((bf16[32,32,128]{2,1,0:T(8,128)(2,1)}), bf16[32,32,128]{2,1,0:T(8,128)(2,1)S(1)}, u32[]{:S(2)}, u32[]{:S(2)}) %all-to-all-start.1) | async-done | bytes 262176 | tf_op jit(solution)/shard_map/all_to_all | solution.py:386
  66.4 2.9 %shard_map.145 = f32[2048,128]{1,0:T(8,128)} custom-call(s32[16,4]{1,0:T(8,128)S(1)} %copy.18.dst, bf16[32,32,128]{2,1,0:T(8,128)(2,1)S(1)} %all-to-all-done.1.arrived, f32[2048,128]{1,0:T(8,128)S(1)} %get-tuple-element.27.land_flux), custom_call_target="tpu_custom_call" | custom-call | flops 10000000 | bytes 2500000 | tf_op jit(solution)/shard_map/pallas_call | solution.py:319
  (21 shorter events, 0.0 us)
Async XLA Ops:
  0.6 13.5 %copy-start.22 = (s32[1,16,4]{1,2,0:T(4,128)S(1)}, s32[1,16,4]{1,2,0:T(4,128)}, u32[]{:S(2)}) copy-start(s32[1,16,4]{1,2,0:T(4,128)} %param.19) | copy-start | bytes 772
  0.6 13.6 %copy-start.23 = (s32[16,1,4]{0,2,1:T(4,128)S(1)}, s32[16,1,4]{0,2,1:T(4,128)}, u32[]{:S(2)}) copy-start(s32[16,1,4]{0,2,1:T(4,128)} %param.22) | copy-start | bytes 772
  1.4 1.6 %copy-start = (f32[1,16,32,1024]{3,2,1,0:T(8,128)S(1)}, f32[1,16,32,1024]{3,2,1,0:T(8,128)}, u32[]{:S(2)}) copy-start(f32[1,16,32,1024]{3,2,1,0:T(8,128)} %param.13) | copy-start | bytes 6291460
  3.0 11.3 %copy-start.1 = (f32[1,16,32,1024]{3,2,1,0:T(8,128)S(1)}, f32[1,16,32,1024]{3,2,1,0:T(8,128)}, u32[]{:S(2)}) copy-start(f32[1,16,32,1024]{3,2,1,0:T(8,128)} %param.13) | copy-start | bytes 6291460
  5.2 31.4 %all-to-all-start = ((bf16[32,32,128]{2,1,0:T(8,128)(2,1)}), bf16[32,32,128]{2,1,0:T(8,128)(2,1)S(1)}, u32[]{:S(2)}, u32[]{:S(2)}) async-start(bf16[32,32,128]{2,1,0:T(8,128)(2,1)} %get-tuple-element.15), calls=%async_computation | async-start | bytes 524288 | tf_op jit(solution)/shard_map/all_to_all | solution.py:360
  12.6 10.4 %collective-permute-start = (f32[256,128]{1,0:T(8,128)}, f32[256,128]{1,0:T(8,128)}, u32[]{:S(2)}, u32[]{:S(2)}) collective-permute-start(f32[256,128]{1,0:T(8,128)} %get-tuple-element.17), channel_id=1, source_target_pairs={{0,1},{1,0},{2,3},{3,2},{4,5},{5,4},{6,7},{7,6},{8,9},{9,8},{10,11... | collective-permute-start | bytes 393224 | tf_op jit(solution)/shard_map/ppermute | solution.py:361
  12.9 10.1 %collective-permute-start.1 = (f32[256,128]{1,0:T(8,128)}, f32[256,128]{1,0:T(8,128)}, u32[]{:S(2)}, u32[]{:S(2)}) collective-permute-start(f32[256,128]{1,0:T(8,128)} %get-tuple-element.18), channel_id=1, source_target_pairs={{1,2},{3,4},{5,6},{7,8},{9,10},{11,12},{13,14},{2,1},{4,3},{6,5},{... | collective-permute-start | bytes 393224 | tf_op jit(solution)/shard_map/ppermute | solution.py:363
  14.3 1.6 %copy-start.2 = (bf16[16,1,4,128,128]{4,3,2,1,0:T(8,128)(2,1)S(1)}, bf16[16,1,4,128,128]{4,3,2,1,0:T(8,128)(2,1)}, u32[]{:S(2)}) copy-start(bf16[16,1,4,128,128]{4,3,2,1,0:T(8,128)(2,1)} %param.25) | copy-start | bytes 6291460
  15.9 1.2 %copy-start.9 = (f32[8,32,1024]{2,1,0:T(8,128)S(1)}, f32[8,32,1024]{2,1,0:T(8,128)}, u32[]{:S(2)}) copy-start(f32[8,32,1024]{2,1,0:T(8,128)} %param.17) | copy-start | bytes 3145732
  17.2 0.7 copy-start.19
  17.8 5.1 %copy-start.24 = (f32[1,16]{1,0:T(1,128)S(1)}, f32[1,16]{1,0:T(1,128)}, u32[]{:S(2)}) copy-start(f32[1,16]{1,0:T(1,128)} %param.14) | copy-start | bytes 196
  17.8 5.2 %copy-start.14 = (s32[1,32,1024]{2,1,0:T(8,128)S(1)}, s32[1,32,1024]{2,1,0:T(8,128)}, u32[]{:S(2)}) copy-start(s32[1,32,1024]{2,1,0:T(8,128)} %mask.3) | copy-start | bytes 393220
  17.8 5.2 %copy-start.18 = (f32[1,16,16]{2,1,0:T(8,128)S(1)}, f32[1,16,16]{2,1,0:T(8,128)}, u32[]{:S(2)}) copy-start(f32[1,16,16]{2,1,0:T(8,128)} %param.15) | copy-start | bytes 3076
  21.3 1.0 %copy-start.10 = (f32[2048,128]{1,0:T(8,128)}, f32[2048,128]{1,0:T(8,128)S(1)}, u32[]{:S(2)}) copy-start(f32[2048,128]{1,0:T(8,128)S(1)} %get-tuple-element.20.lagged) | copy-start | bytes 3145732
  22.3 0.6 copy-start.16
  22.9 13.7 %copy-start.3 = (bf16[16,1,4,128,128]{4,3,2,1,0:T(8,128)(2,1)S(1)}, bf16[16,1,4,128,128]{4,3,2,1,0:T(8,128)(2,1)}, u32[]{:S(2)}) copy-start(bf16[16,1,4,128,128]{4,3,2,1,0:T(8,128)(2,1)} %param.25) | copy-start | bytes 6291460
  35.6 1.0 %copy-start.12 = (f32[2048,128]{1,0:T(8,128)}, f32[2048,128]{1,0:T(8,128)S(1)}, u32[]{:S(2)}) copy-start(f32[2048,128]{1,0:T(8,128)S(1)} %get-tuple-element.19.base) | copy-start | bytes 3145732
  36.6 1.6 %copy-start.4 = (bf16[1,16,4,128,128]{4,3,2,1,0:T(8,128)(2,1)S(1)}, bf16[1,16,4,128,128]{4,3,2,1,0:T(8,128)(2,1)}, u32[]{:S(2)}) copy-start(bf16[1,16,4,128,128]{4,3,2,1,0:T(8,128)(2,1)} %param.21) | copy-start | bytes 6291460
  38.2 1.2 %copy-start.11 = (f32[2048,128]{1,0:T(8,128)S(1)}, f32[2048,128]{1,0:T(8,128)}, u32[]{:S(2)}) copy-start(f32[2048,128]{1,0:T(8,128)} %copy-done.10) | copy-start | bytes 3145732
  39.4 1.2 %copy-start.13 = (f32[2048,128]{1,0:T(8,128)S(1)}, f32[2048,128]{1,0:T(8,128)}, u32[]{:S(2)}) copy-start(f32[2048,128]{1,0:T(8,128)} %copy-done.12) | copy-start | bytes 3145732
  40.7 0.8 %copy-start.17 = (f32[16,8,128]{2,1,0:T(8,128)S(1)}, f32[16,8,128]{2,1,0:T(8,128)}, u32[]{:S(2)}) copy-start(f32[16,8,128]{2,1,0:T(8,128)} %copy-done.16) | copy-start | bytes 196612
  41.5 0.7 copy-start.20
  42.2 0.7 copy-start.21
  46.7 1.0 %copy-start.5 = (f32[2048,128]{1,0:T(8,128)}, f32[2048,128]{1,0:T(8,128)S(1)}, u32[]{:S(2)}) copy-start(f32[2048,128]{1,0:T(8,128)S(1)} %get-tuple-element.22.top) | copy-start | bytes 3145732
  47.7 1.0 %copy-start.7 = (f32[2048,128]{1,0:T(8,128)}, f32[2048,128]{1,0:T(8,128)S(1)}, u32[]{:S(2)}) copy-start(f32[2048,128]{1,0:T(8,128)S(1)} %get-tuple-element.24.flux) | copy-start | bytes 3145732
  48.6 0.7 copy-start.15
  49.3 17.1 %all-to-all-start.1 = ((bf16[32,32,128]{2,1,0:T(8,128)(2,1)}), bf16[32,32,128]{2,1,0:T(8,128)(2,1)S(1)}, u32[]{:S(2)}, u32[]{:S(2)}) async-start(bf16[32,32,128]{2,1,0:T(8,128)(2,1)} %copy-done.15), calls=%async_computation.1 | async-start | bytes 524288 | tf_op jit(solution)/shard_map/all_to_all | solution.py:386
  56.9 1.2 %copy-start.6 = (f32[2048,128]{1,0:T(8,128)S(1)}, f32[2048,128]{1,0:T(8,128)}, u32[]{:S(2)}) copy-start(f32[2048,128]{1,0:T(8,128)} %copy-done.5) | copy-start | bytes 3145732
  58.2 1.2 %copy-start.8 = (f32[2048,128]{1,0:T(8,128)S(1)}, f32[2048,128]{1,0:T(8,128)}, u32[]{:S(2)}) copy-start(f32[2048,128]{1,0:T(8,128)} %copy-done.7) | copy-start | bytes 3145732

commit v2 on v1

v2 whole, which is shorter than its diff:
```python
import functools

import jax
import jax.numpy as jnp
from jax import lax
from jax.experimental import pallas as pl
from jax.experimental.pallas import tpu as pltpu
from jax.sharding import PartitionSpec as P

NF = 8
BLK = 128
CAP = 4
NSUB = 2
SUB = 8
F32 = jnp.float32
BF16 = jnp.bfloat16
VMEM_LIMIT = 12 * 1024 * 1024


def tile_view(grid):
    levels, rows, cells = grid.shape
    split = grid.reshape(levels, rows // SUB, SUB, cells // BLK, BLK)
    return split.transpose(0, 1, 3, 2, 4).reshape(levels * rows * cells // BLK, BLK)


def from_tile_view(tiles, levels, rows, cells):
    split = tiles.reshape(levels, rows // SUB, cells // BLK, SUB, BLK)
    return split.transpose(0, 1, 3, 2, 4).reshape(levels, rows, cells)


def tile_row(row, x, columns):
    return (lax.div(row, SUB) * columns + x) * SUB + lax.rem(row, SUB)


def block_tile_row(block, columns):
    return tile_row(lax.div(block, columns), lax.rem(block, columns), columns)


def aligned(index, step):
    return pl.multiple_of(index * step, step)


def loop(count, body, unroll=1):
    def step(i, carry):
        body(i)
        return carry

    lax.fori_loop(0, count, step, 0, unroll=min(unroll, count))


class Copies:
    def __init__(self, semaphores):
        self.semaphores, self.open, self.used = semaphores, {}, 0

    def start(self, name, source, target):
        copy = pltpu.make_async_copy(source, target, self.semaphores.at[self.used])
        self.used += 1
        copy.start()
        self.open[name] = copy

    def wait(self, *names):
        for name in names:
            self.open.pop(name).wait()

    def wait_all(self):
        self.wait(*list(self.open))


def parts_of(count, parts):
    parts = parts if count % parts == 0 else 1
    return [pl.ds(i * (count // parts), count // parts) for i in range(parts)]


def pick_kernel(dims, src_in, state_in, sent_out, slab_a_out, slab_b_out, src, state, sent, slab_a, slab_b, sems):
    rows, columns, levels, tiles = dims
    copies = Copies(sems)
    level_stride = rows * columns
    copies.start("src", src_in, src)
    for i, part in enumerate(parts_of(NF * level_stride, 4)):
        copies.start(("top", i), state_in.at[part], state.at[part])
    deep = pl.ds(NF * level_stride, (levels - NF) * level_stride)
    copies.start("deep", state_in.at[deep], state.at[deep])
    comp, tile = lax.axis_index("comp"), lax.axis_index("tile")
    other = (1 - comp) * tiles

    def blank(t):
        sent[comp * tiles + t] = jnp.zeros((CAP * NF, BLK), BF16)

    loop(tiles, blank, unroll=16)

    def one_tile(t):
        for pair in range(CAP // 2):
            two = []
            for k in (2 * pair, 2 * pair + 1):
                start = block_tile_row(src[k, t], columns)
                two.append(state[pl.ds(start, NF, stride=level_stride), :])
            both = jnp.concatenate(two, axis=0).astype(BF16)
            sent[other + t, pl.ds(2 * NF * pair, 2 * NF), :] = both

    copies.wait("src", *[("top", i) for i in range(len(parts_of(NF * level_stride, 4)))])
    loop(tiles, one_tile, unroll=16)
    for name, half in (("sent", other), ("own", comp * tiles)):
        where = pl.ds(half, tiles)
        copies.start(name, sent.at[where], sent_out.at[where])
    even = lax.rem(tile, 2) == 0
    copies.wait("deep")
    for slab, first in (
        (slab_a, jnp.where(even, rows - NSUB, 0)),
        (slab_b, jnp.where(even, 0, rows - NSUB)),
    ):
        for i in range(NSUB):
            for x in range(columns):
                start = tile_row(first + i, x, columns)
                value = state[pl.ds(start, levels, stride=level_stride), :]
                slab[(i * columns + x) * levels : (i * columns + x + 1) * levels, :] = value
    copies.start("a", slab_a, slab_a_out)
    copies.start("b", slab_b, slab_b_out)
    copies.wait_all()


def prepare_kernel(
    dims, count_in, state_in, lagged_in, weight_in, blocks, lagged_out, sums_out,
    count, state, lagged, weight, lagged_blocks, column_sums, sems,
):
    rows, columns, levels, tiles = dims
    copies = Copies(sems)
    level_stride = rows * columns
    for i, part in enumerate(parts_of(levels * level_stride, 4)):
        copies.start(("state", i), state_in.at[part], state.at[part])
    copies.start("count", count_in, count)
    for i, part in enumerate(parts_of(NF * level_stride, 2)):
        copies.start(("lagged", i), lagged_in.at[part], lagged.at[part])
    for i, part in enumerate(parts_of(tiles, 4)):
        copies.start(("weight", i), weight_in.at[part], weight.at[part])
    comp = lax.axis_index("comp")
    atmosphere = jnp.where(comp == 0, 1.0, 0.0).astype(F32)

    def one_row(r):
        for x in range(columns):
            start = tile_row(r, x, columns)
            block = r * columns + x
            blocks[pl.ds(aligned(block, levels), levels), :] = state[
                pl.ds(start, levels, stride=level_stride), :
            ]

    def lagged_row(r):
        for x in range(columns):
            start = tile_row(r, x, columns)
            lagged_blocks[pl.ds(aligned(r * columns + x, NF), NF), :] = (
                lagged[pl.ds(start, NF, stride=level_stride), :] * atmosphere
            )

    copies.wait(*[("state", i) for i in range(len(parts_of(levels * level_stride, 4)))])
    loop(rows, one_row, unroll=32)
    copies.wait(*[("lagged", i) for i in range(len(parts_of(NF * level_stride, 2)))])
    loop(rows, lagged_row, unroll=32)
    copies.start("lagged_blocks", lagged_blocks, lagged_out)
    ones = jnp.ones((2 * SUB, BLK), BF16)
    rows_of = lax.broadcasted_iota(jnp.int32, (SUB, BLK), 0)
    copies.wait("count")

    def one_tile(t):
        live = count[t]
        sums = jnp.zeros((SUB, BLK), F32)
        for k in range(CAP):
            column = jnp.dot(ones, weight[t, k], preferred_element_type=F32)[:SUB]
            column = column * jnp.where(k < live, 1.0, 0.0).astype(F32)
            sums = jnp.where((rows_of == k) | (rows_of == k + CAP), column, sums)
        high = sums.astype(BF16).astype(F32)
        column_sums[t] = jnp.where(rows_of < CAP, high, sums - high)

    for i, part in enumerate(parts_of(tiles, 4)):
        copies.wait(("weight", i))
        loop(part.size, lambda t, part=part: one_tile(part.start + t), unroll=16)
    copies.start("sums", column_sums, sums_out)
    copies.wait_all()


def diffuse_kernel(
    dims, blocks, kappa, col_mix, from_a_in, from_b_in, mask_in, base_out, deep_out,
    from_a, from_b, mask, base, deep, stepped, sems,
):
    rows, columns, levels, tiles = dims
    copies = Copies(sems)
    copies.start("a", from_a_in, from_a)
    copies.start("b", from_b_in, from_b)
    copies.start("mask", mask_in, mask)
    tile = lax.axis_index("tile")
    even = lax.rem(tile, 2) == 0
    above_in = jnp.where(tile > 0, 1.0, 0.0).astype(F32)
    below_in = jnp.where(tile < tiles - 1, 1.0, 0.0).astype(F32)
    rate = kappa[...]
    keep = 1.0 - 4.0 * rate
    lane = lax.broadcasted_iota(jnp.int32, (levels, BLK), 1)

    def load_row(ref, r):
        return [
            ref[pl.ds(aligned(r * columns + x, levels), levels), :] for x in range(columns)
        ]

    def slab_row(above, i):
        first, second = (from_b, from_a) if above else (from_a, from_b)
        return [
            jnp.where(even, p, q)
            for p, q in zip(load_row(first, i), load_row(second, i), strict=True)
        ]

    def stencil(up, mid, down):
        right_roll = [pltpu.roll(v, 1, 1) for v in mid]
        left_roll = [pltpu.roll(v, BLK - 1, 1) for v in mid]
        out = []
        for x in range(columns):
            west = jnp.where(lane == 0, right_roll[x - 1], right_roll[x])
            east = jnp.where(lane == BLK - 1, left_roll[(x + 1) % columns], left_roll[x])
            out.append(keep * mid[x] + rate * (up[x] + down[x] + (west + east)))
        return out

    def store_stepped(r, values, scale=None):
        for x, v in enumerate(values):
            v = v if scale is None else v * scale
            stepped[pl.ds(aligned((r + 1) * columns + x, levels), levels), :] = v

    def first_step(i):
        r = i + 1
        store_stepped(
            r, stencil(load_row(blocks, r - 1), load_row(blocks, r), load_row(blocks, r + 1))
        )

    loop(rows - 2, first_step, unroll=30)
    copies.wait("a", "b")
    above = [slab_row(True, i) for i in range(NSUB)]
    store_stepped(-1, stencil(above[0], above[1], load_row(blocks, 0)), above_in)
    store_stepped(0, stencil(above[1], load_row(blocks, 0), load_row(blocks, 1)))
    below = [slab_row(False, i) for i in range(NSUB)]
    store_stepped(
        rows - 1, stencil(load_row(blocks, rows - 2), load_row(blocks, rows - 1), below[0])
    )
    store_stepped(rows, stencil(load_row(blocks, rows - 1), below[0], below[1]), below_in)
    mix = col_mix[...]
    mix_high = mix.astype(BF16)
    mix_low = (mix - mix_high.astype(F32)).astype(BF16)
    mix_three = jnp.concatenate([mix_high, mix_high, mix_low], axis=1)
    copies.wait("mask")

    def second_step(r):
        done = stencil(load_row(stepped, r), load_row(stepped, r + 1), load_row(stepped, r + 2))
        whole = jnp.concatenate(done, axis=1)
        high = whole.astype(BF16)
        low = (whole - high.astype(F32)).astype(BF16)
        three = jnp.concatenate([high, low, high], axis=0)
        mixed = jnp.dot(mix_three, three, preferred_element_type=F32)
        moved = whole + 0.5 * jnp.tanh(mixed)
        land = mask[0, pl.ds(r, 1), :].astype(F32)
        top = moved[:NF] - (0.5 * (1.0 - land)) * whole[:NF]
        rest = moved[NF:]
        for x in range(columns):
            where = r * columns + x
            cells = slice(x * BLK, (x + 1) * BLK)
            base[pl.ds(aligned(where, NF), NF), :] = top[:, cells]
            deep[pl.ds(aligned(where, levels - NF), levels - NF), :] = rest[:, cells]

    for i, part in enumerate(parts_of(rows, 2)):
        loop(part.size, lambda r, part=part: second_step(part.start + r), unroll=16)
        for name, source, target, depth in (
            ("base", base, base_out, NF), ("deep", deep, deep_out, levels - NF),
        ):
            where = pl.ds(part.start * columns * depth, part.size * columns * depth)
            copies.start((name, i), source.at[where], target.at[where])
    copies.wait_all()


def surface_kernel(
    dims, arrived, dst_in, live_in_in, src_in, live_out_in, weight_in_in, base_in, lagged_in, mask_in, weight_out_in,
    sums_in, sent_out, top_out, flux_out,
    dst, live_in, src, live_out, weight_in, base, lagged, mask, weight_out, column_sums, sent, top, flux,
    numerator, denominator, sems,
):
    rows, columns, _, tiles = dims
    copies = Copies(sems)
    copies.start("dst", dst_in, dst)
    copies.start("live_in", live_in_in, live_in)
    tile_parts = parts_of(tiles, 4)
    for i, part in enumerate(tile_parts):
        copies.start(("weight_in", i), weight_in_in.at[part], weight_in.at[part])
    copies.start("base", base_in, base)
    copies.start("lagged", lagged_in, lagged)
    copies.start("mask", mask_in, mask)
    copies.start("src", src_in, src)
    copies.start("live_out", live_out_in, live_out)
    copies.start("sums", sums_in, column_sums)
    for i, part in enumerate(tile_parts):
        copies.start(("weight_out", i), weight_out_in.at[part], weight_out.at[part])
    comp = lax.axis_index("comp")
    other, own = (1 - comp) * tiles, comp * tiles

    def clear(r):
        for x in range(columns):
            where = pl.ds(aligned(r * columns + x, NF), NF)
            numerator[where, :] = jnp.zeros((NF, BLK), F32)
            denominator[where, :] = jnp.zeros((NF, BLK), F32)

    loop(rows, clear, unroll=32)
    ones = jnp.ones((NF, BLK), F32)

    def receive(t):
        got = arrived[other + t].astype(F32)
        for k in range(CAP):
            both = jnp.concatenate([got[k * NF : (k + 1) * NF], ones], axis=0).astype(BF16)
            product = jnp.dot(both, weight_in[t, k], preferred_element_type=F32)
            live = jnp.where(k < live_in[t], 1.0, 0.0).astype(F32)
            product = product * live
            where = pl.ds(aligned(dst[k, t], NF), NF)
            numerator[where, :] += product[:NF]
            denominator[where, :] += product[NF:]

    copies.wait("dst", "live_in")
    for i, part in enumerate(tile_parts):
        copies.wait(("weight_in", i))
        loop(part.size, lambda t, part=part: receive(part.start + t), unroll=16)
    copies.wait("base", "lagged", "mask")

    def one_row(r):
        land_row = mask[0, pl.ds(r, 1), :].astype(F32)
        for x in range(columns):
            where = pl.ds(aligned(r * columns + x, NF), NF)
            land = land_row[:, x * BLK : (x + 1) * BLK]
            received = numerator[where, :] / jnp.maximum(denominator[where, :], 1.0)
            incoming = lagged[where, :] + received
            state = base[where, :] + land * incoming
            top[where, :] = state
            flux[where, :] = land * jnp.tanh(state - incoming)

    loop(rows, one_row, unroll=32)
    copies.start("top", top, top_out)
    copies.start("flux", flux, flux_out)

    def send(t):
        for pair in range(CAP // 2):
            two = []
            for k in (2 * pair, 2 * pair + 1):
                picked = flux[pl.ds(aligned(src[k, t], NF), NF), :].astype(BF16)
                product = jnp.dot(picked, weight_out[t, k], preferred_element_type=F32)
                two.append(product * jnp.where(k < live_out[t], 1.0, 0.0).astype(F32))
            both = jnp.concatenate(two, axis=0).astype(BF16)
            sent[other + t, pl.ds(2 * NF * pair, 2 * NF), :] = both
        sums = jnp.concatenate([column_sums[t], jnp.zeros((SUB, BLK), F32)], axis=0)
        sent[own + t, pl.ds(0, 2 * SUB), :] = sums.astype(BF16)
        sent[own + t, pl.ds(2 * SUB, 2 * SUB), :] = jnp.zeros((2 * SUB, BLK), BF16)

    copies.wait("src", "live_out", "sums")
    for i, part in enumerate(tile_parts):
        copies.wait(("weight_out", i))
        loop(part.size, lambda t, part=part: send(part.start + t), unroll=16)
        for half in (other, own):
            where = pl.ds(half + part.start, part.size)
            copies.start(("sent", i, half is own), sent.at[where], sent_out.at[where])
    copies.wait_all()


def write_kernel(dims, top_in, deep_in, flux_in, new_state_out, land_flux_out, top, deep, flux, new_state, land_flux, sems):
    rows, columns, levels, _ = dims
    copies = Copies(sems)
    copies.start("top", top_in, top)
    copies.start("deep", deep_in, deep)
    copies.start("flux", flux_in, flux)
    comp = lax.axis_index("comp")
    on_land = jnp.where(comp == 1, 1.0, 0.0).astype(F32)
    depth = levels - NF
    cut = NF * rows * columns

    def from_blocks(source, target, count, first, scale=None):
        def one(rt):
            for x in range(columns):
                for level in range(count):
                    out = ((level + first) * (rows // SUB) + rt) * columns + x
                    start = (rt * SUB * columns + x) * count + level
                    value = source[pl.ds(start, SUB, stride=columns * count), :]
                    value = value if scale is None else value * scale
                    target[pl.ds(aligned(out, SUB), SUB), :] = value

        loop(rows // SUB, one, unroll=4)

    copies.wait("top")
    from_blocks(top, new_state, NF, 0)
    copies.start("state", new_state.at[pl.ds(0, cut)], new_state_out.at[pl.ds(0, cut)])
    copies.wait("deep")
    from_blocks(deep, new_state, depth, NF)
    rest = pl.ds(cut, depth * rows * columns)
    copies.start("rest", new_state.at[rest], new_state_out.at[rest])
    copies.wait("flux")
    from_blocks(flux, land_flux, NF, 0, on_land)
    copies.start("land", land_flux, land_flux_out)
    copies.wait_all()


def return_kernel(dims, arrived, dst_in, land_flux_in, fluxes_out, dst, land_flux, fluxes, numerator, denominator, sems):
    rows, columns, _, tiles = dims
    copies = Copies(sems)
    copies.start("dst", dst_in, dst)
    halves = parts_of(NF * rows * columns, 2)
    for i, part in enumerate(halves):
        copies.start(("land", i), land_flux_in.at[part], land_flux.at[part])
        copies.start(("fluxes", i), land_flux_in.at[part], fluxes.at[part])
    comp = lax.axis_index("comp")
    other = (1 - comp) * tiles
    level_stride = rows * columns

    def clear(r):
        for x in range(columns):
            where = pl.ds(aligned(r * columns + x, NF), NF)
            numerator[where, :] = jnp.zeros((NF, BLK), F32)
            denominator[where, :] = jnp.zeros((NF, BLK), F32)

    loop(rows, clear, unroll=32)

    def receive(t):
        got = arrived[other + t].astype(F32)
        sums = arrived[comp * tiles + t].astype(F32)
        sums = sums[:CAP] + sums[CAP : 2 * CAP]
        for k in range(CAP):
            where = pl.ds(aligned(dst[k, t], NF), NF)
            numerator[where, :] += got[k * NF : (k + 1) * NF]
            denominator[where, :] += jnp.broadcast_to(sums[k : k + 1], (NF, BLK))

    copies.wait("dst")
    loop(tiles, receive, unroll=16)
    copies.wait_all()

    def finish(t):
        for k in range(CAP):
            block = dst[k, t]
            where = pl.ds(aligned(block, NF), NF)
            out = pl.ds(block_tile_row(block, columns), NF, stride=level_stride)
            value = numerator[where, :] / jnp.maximum(denominator[where, :], 1.0)
            fluxes[out, :] = land_flux[out, :] + value

    loop(tiles, finish, unroll=16)
    for i, part in enumerate(halves):
        copies.start(("out", i), fluxes.at[part], fluxes_out.at[part])
    copies.wait_all()


def call(kernel, operands, places, outs, scratch, copies, limit, cost):
    spec = {"v": pl.BlockSpec(memory_space=pltpu.VMEM), "h": pl.BlockSpec(memory_space=pltpu.HBM)}
    operands = [
        pltpu.with_memory_space_constraint(x, pltpu.HBM) if place == "h" else x
        for x, place in zip(operands, places, strict=True)
    ]
    return pl.pallas_call(
        kernel,
        out_shape=[out for out, _ in outs],
        in_specs=[spec[place] for place in places],
        out_specs=[spec[place] for _, place in outs],
        scratch_shapes=[*scratch, pltpu.SemaphoreType.DMA((copies,))],
        compiler_params=pltpu.CompilerParams(vmem_limit_bytes=limit),
        cost_estimate=pl.CostEstimate(flops=cost, bytes_accessed=cost // 4, transcendentals=0),
    )(*operands)


def per_device(
    state,
    kappa,
    col_mix,
    surface_mask,
    lagged_flux,
    a2l_src,
    a2l_dst,
    a2l_count,
    a2l_weight,
    l2a_src,
    l2a_dst,
    l2a_count,
    l2a_weight,
):
    fields = state[0]
    levels, rows, cells = fields.shape
    columns = cells // BLK
    nblocks = rows * columns
    tiles = lax.axis_size("tile")
    dims = (rows, columns, levels, tiles)
    shape, vmem, smem = pltpu.HBM, pltpu.VMEM, pltpu.SMEM
    kernel = lambda f: functools.partial(f, dims)
    limit = VMEM_LIMIT + 4 * tiles * CAP * BLK * BLK
    state_tiles = tile_view(fields)
    slab = (NSUB * columns * levels, BLK)
    parcel = (2 * tiles, CAP * NF, BLK)
    top_shape = (nblocks * NF, BLK)
    deep_shape = (nblocks * (levels - NF), BLK)
    full_shape = (nblocks * levels, BLK)
    sums_shape = (tiles, SUB, BLK)
    weight_shape = (tiles, CAP, BLK, BLK)
    slots, counts = smem((CAP, tiles), jnp.int32), smem((tiles,), jnp.int32)
    sent, slab_a, slab_b = call(
        kernel(pick_kernel), [a2l_src[:, 0, :].T, state_tiles], "hh",
        [(shape(parcel, BF16), "h"), (shape(slab, F32), "h"), (shape(slab, F32), "h")],
        [slots, vmem(full_shape, F32), vmem(parcel, BF16), vmem(slab, F32), vmem(slab, F32)],
        10, limit, 4_000_000,
    )
    arrived = lax.all_to_all(sent, ("comp", "tile"), split_axis=0, concat_axis=0, tiled=True)
    from_a = lax.ppermute(slab_a, "tile", [(i, i ^ 1) for i in range(tiles)])
    pairs = [(i, i + 1) for i in range(1, tiles - 1, 2)]
    from_b = lax.ppermute(slab_b, "tile", pairs + [(j, i) for i, j in pairs])
    blocks, lagged_blocks, column_sums = call(
        kernel(prepare_kernel),
        [l2a_count[:, 0], state_tiles, tile_view(lagged_flux), l2a_weight[:, 0]], "hhhh",
        [(vmem(full_shape, F32), "v"), (shape(top_shape, F32), "h"), (shape(sums_shape, F32), "h")],
        [counts, vmem(full_shape, F32), vmem(top_shape, F32), vmem(weight_shape, BF16),
         vmem(top_shape, F32), vmem(sums_shape, F32)],
        13, limit, 20_000_000,
    )
    base, deep = call(
        kernel(diffuse_kernel),
        [blocks, jnp.broadcast_to(kappa[0][:, None], (levels, BLK)), col_mix[0], from_a, from_b,
         surface_mask], "vvvhhh",
        [(shape(top_shape, F32), "h"), (shape(deep_shape, F32), "h")],
        [vmem(slab, F32), vmem(slab, F32), vmem((1, rows, cells), jnp.int32), vmem(top_shape, F32),
         vmem(deep_shape, F32), vmem(((rows + 2) * columns * levels, BLK), F32)],
        7, limit, 20_000_000,
    )
    sent_back, top, flux = call(
        kernel(surface_kernel),
        [arrived, a2l_dst[0].T, a2l_count[0], l2a_src[:, 0, :].T, l2a_count[:, 0], a2l_weight[0], base,
         lagged_blocks, surface_mask, l2a_weight[:, 0], column_sums], "vhhhhhhhhhh",
        [(shape(parcel, BF16), "h"), (shape(top_shape, F32), "h"), (shape(top_shape, F32), "h")],
        [slots, counts, slots, counts, vmem(weight_shape, BF16), vmem(top_shape, F32),
         vmem(top_shape, F32), vmem((1, rows, cells), jnp.int32), vmem(weight_shape, BF16),
         vmem(sums_shape, F32), vmem(parcel, BF16), vmem(top_shape, F32), vmem(top_shape, F32),
         vmem(top_shape, F32), vmem(top_shape, F32)],
        26, limit, 20_000_000,
    )
    returned = lax.all_to_all(
        sent_back, ("comp", "tile"), split_axis=0, concat_axis=0, tiled=True
    )
    new_state, land_flux = call(
        kernel(write_kernel), [top, deep, flux], "hhh",
        [(shape(full_shape, F32), "h"), (shape(top_shape, F32), "h")],
        [vmem(top_shape, F32), vmem(deep_shape, F32), vmem(top_shape, F32), vmem(full_shape, F32),
         vmem(top_shape, F32)],
        6, limit, 20_000_000,
    )
    (fluxes,) = call(
        kernel(return_kernel), [returned, l2a_dst[0].T, land_flux], "vhh",
        [(shape(top_shape, F32), "h")],
        [slots, vmem(top_shape, F32), vmem(top_shape, F32), vmem(top_shape, F32), vmem(top_shape, F32)],
        7, limit, 10_000_000,
    )
    return (
        from_tile_view(new_state, levels, rows, cells)[None],
        from_tile_view(fluxes, NF, rows, cells)[None],
    )


def solution(mesh):
    return jax.shard_map(
        per_device,
        mesh=mesh,
        in_specs=(
            P("comp", None, "tile", None),
            P("comp", None),
            P("comp", None, None),
            P("comp", "tile", None),
            P(None, "tile", None),
            P(None, "tile", None),
            P("tile", None, None),
            P("tile", None),
            P("tile", None, None, None, None),
            P(None, "tile", None),
            P("tile", None, None),
            P(None, "tile"),
            P(None, "tile", None, None, None),
        ),
        out_specs=(P("comp", None, "tile", None), P("comp", None, "tile", None)),
        check_vma=False,
    )
```

time: 70 us -> 46.9 us (0.67)
  local copies, waits for them, and re-layouts: 20.7 us -> 0.69 us
  Pallas kernels: 28.2 us -> 23.2 us
  waiting for transfers between devices: 3.92 us -> 6.15 us
    unnamed x50 -> x8, local copies, waits for them, and re-layouts: 18.9 us -> 0.62 us
    pallas_call x6, Pallas kernels: 28.2 us -> 23.2 us  [call(): pl.pallas_call(kernel, out_shape=[out for out, _ in outs], in_specs=[spec...]
    all_to_all x1, waiting for transfers between devices: 3.92 us -> 6.14 us  [per_device(): lax.all_to_all(sent_back, ('comp', 'tile'), split_axis=0, concat_axis=0,...]
    squeeze x4 -> x0, local copies, waits for them, and re-layouts: 1.7 us -> none  [the longest x1 0.77 us: per_device(): a2l_src[:, 0, :]]
  transfers between devices with their start and end apart: 4 -> 4, of which waited for: 1 -> 1; matrix products, arithmetic and copies ran while one was open for 1% -> 0% of each run, Pallas kernels for 28% -> 28%
where the time goes in v2:
time: 46.9 us; the launch traced here: 46.6 us
  Pallas kernels  23.2 us (49%)
  starting transfers between devices  15.8 us (34%)
  waiting for transfers between devices  6.15 us (13%)
  between operations  0.76 us (2%)
  local copies, waits for them, and re-layouts  0.69 us (1%)
    pallas_call x6, Pallas kernels, call(): pl.pallas_call(kernel, out_shape=[out for out, _ in outs], in_specs=[spec...  23.2 us
    all_to_all x1, starting transfers between devices, per_device(): lax.all_to_all(sent_back, ('comp', 'tile'), split_axis=0, concat_axis=0,...  7.47 us
    all_to_all x1, starting transfers between devices, per_device(): lax.all_to_all(sent, ('comp', 'tile'), split_axis=0, concat_axis=0, tiled...  7.33 us
    all_to_all x1, waiting for transfers between devices, per_device(): lax.all_to_all(sent_back, ('comp', 'tile'), split_axis=0, concat_axis=0,...  6.14 us
  transfers between devices with their start and end apart: 4, of which 1 were waited for; matrix products, arithmetic and copies ran while one was open for 0% of the time, Pallas kernels for 28%

profile of v2, /device:TPU:0, one launch (start us, length us, event | category | flops | bytes accessed | tf_op | source)
XLA Modules:
  0.0 46.6 jit_solution(2200216613341680906)
XLA Ops:
  0.6 2.5 %shard_map.140 = (bf16[32,32,128]{2,1,0:T(8,128)(2,1)}, f32[256,128]{1,0:T(8,128)}, f32[256,128]{1,0:T(8,128)}) custom-call(s32[4,16]{1,0:T(4,128)} %bitcast.48, f32[4096,128]{1,0:T(8,128)} %bitcast.41), custom_call_target="tpu_custom_call" | custom-call | flops 4000000 | bytes 1000000 | tf_op jit(solution)/shard_map/pallas_call | solution.py:449
  3.2 7.3 %all-to-all-start = ((bf16[32,32,128]{2,1,0:T(8,128)(2,1)}), bf16[32,32,128]{2,1,0:T(8,128)(2,1)S(1)}, u32[]{:S(2)}, u32[]{:S(2)}) async-start(bf16[32,32,128]{2,1,0:T(8,128)(2,1)} %get-tuple-element.15), calls=%async_computation | async-start | bytes 524288 | tf_op jit(solution)/shard_map/all_to_all | solution.py:499
  10.5 0.3 collective-permute-start
  10.8 0.7 %collective-permute-start.1 = (f32[256,128]{1,0:T(8,128)}, f32[256,128]{1,0:T(8,128)S(1)}, u32[]{:S(2)}, u32[]{:S(2)}) collective-permute-start(f32[256,128]{1,0:T(8,128)} %get-tuple-element.18), channel_id=1, source_target_pairs={{1,2},{3,4},{5,6},{7,8},{9,10},{11,12},{13,14},{2,1},{4,3},{6,5},{... | collective-permute-start | bytes 393224 | tf_op jit(solution)/shard_map/ppermute | solution.py:502
  11.5 0.0 copy-start.3
  11.5 0.0 copy-start
  11.5 5.1 %shard_map.141 = (f32[4096,128]{1,0:T(8,128)S(1)}, f32[2048,128]{1,0:T(8,128)}, f32[16,8,128]{2,1,0:T(8,128)}) custom-call(s32[16]{0:T(128)} %bitcast.50, f32[4096,128]{1,0:T(8,128)} %bitcast.42, f32[2048,128]{1,0:T(8,128)} %bitcast.45, bf16[16,4,128,128]{3,2,1,0:T(8,128)(2,1)} %bitcast.39), custom_call_target="tpu_custom_call" | custom-call | flops 20000000 | bytes 5000000 | tf_op jit(solution)/shard_map/pallas_call | solution.py:449
  16.6 0.0 collective-permute-done.from_a_in
  16.6 0.0 copy-start.1
  16.7 0.0 collective-permute-done.1.from_b_in
  16.7 0.0 copy-start.2
  16.7 0.0 copy-done.3
  16.7 0.1 broadcast_in_dim.8.kappa
  16.8 0.5 %copy-done.1 = f32[256,128]{1,0:T(8,128)} copy-done((f32[256,128]{1,0:T(8,128)}, f32[256,128]{1,0:T(8,128)S(1)}, u32[]{:S(2)}) %copy-start.1) | copy-done | bytes 131096
  17.3 0.1 copy-done.2
  17.4 0.0 copy-done
  17.4 3.9 %shard_map.142 = (f32[2048,128]{1,0:T(8,128)}, f32[2048,128]{1,0:T(8,128)}) custom-call(f32[4096,128]{1,0:T(8,128)S(1)} %get-tuple-element.16.blocks, f32[16,128]{1,0:T(8,128)S(1)} %broadcast_in_dim.8.kappa, f32[16,16]{1,0:T(8,128)S(1)} %bitcast.38, f32[256,128]{1,0:T(8,128)} %copy-done.1, f32[256,128]{1,0:T(8,128)} %copy-done.2, s32[1,32,1024]{2,1,0:T(8,128)} %mask_in.3), custom_call_target="tpu_custom_call" | custom-call | flops 20000000 | bytes 5000000 | tf_op jit(solution)/shard_map/pallas_call | solution.py:449
  21.2 0.0 all-to-all-done.arrived
  21.3 4.5 %shard_map.143 = (bf16[32,32,128]{2,1,0:T(8,128)(2,1)}, f32[2048,128]{1,0:T(8,128)}, f32[2048,128]{1,0:T(8,128)}) custom-call(bf16[32,32,128]{2,1,0:T(8,128)(2,1)S(1)} %all-to-all-done.arrived, s32[4,16]{1,0:T(4,128)} %bitcast.46, s32[16]{0:T(128)} %bitcast.52, s32[4,16]{1,0:T(4,128)} %bitcast.47, s32[16]{0:T(128)} %bitcast.51, ...), custom_call_target="tpu_custom_call" | custom-call | flops 20000000 | bytes 5000000 | tf_op jit(solution)/shard_map/pallas_call | solution.py:449
  25.8 7.5 %all-to-all-start.1 = ((bf16[32,32,128]{2,1,0:T(8,128)(2,1)}), bf16[32,32,128]{2,1,0:T(8,128)(2,1)S(1)}, u32[]{:S(2)}, u32[]{:S(2)}) async-start(bf16[32,32,128]{2,1,0:T(8,128)(2,1)} %get-tuple-element.26), calls=%async_computation.1 | async-start | bytes 524288 | tf_op jit(solution)/shard_map/all_to_all | solution.py:531
  33.3 4.1 %shard_map.144 = (f32[4096,128]{1,0:T(8,128)}, f32[2048,128]{1,0:T(8,128)}) custom-call(f32[2048,128]{1,0:T(8,128)} %get-tuple-element.22.top_in, f32[2048,128]{1,0:T(8,128)} %get-tuple-element.23.deep_in, f32[2048,128]{1,0:T(8,128)} %get-tuple-element.24.flux_in), custom_call_target="tpu_custom_call" | custom-call | flops 20000000 | bytes 5000000 | tf_op jit(solution)/shard_map/pallas_call | solution.py:449
  37.4 6.1 %all-to-all-done.1.arrived = bf16[32,32,128]{2,1,0:T(8,128)(2,1)S(1)} async-done(((bf16[32,32,128]{2,1,0:T(8,128)(2,1)}), bf16[32,32,128]{2,1,0:T(8,128)(2,1)S(1)}, u32[]{:S(2)}, u32[]{:S(2)}) %all-to-all-start.1) | async-done | bytes 262176 | tf_op jit(solution)/shard_map/all_to_all | solution.py:531
  43.5 3.0 %shard_map.145 = f32[2048,128]{1,0:T(8,128)} custom-call(bf16[32,32,128]{2,1,0:T(8,128)(2,1)S(1)} %all-to-all-done.1.arrived, s32[4,16]{1,0:T(4,128)} %bitcast.49, f32[2048,128]{1,0:T(8,128)} %get-tuple-element.27.land_flux_in), custom_call_target="tpu_custom_call" | custom-call | flops 10000000 | bytes 2500000 | tf_op jit(solution)/shard_map/pallas_call | solution.py:449
Async XLA Ops:
  3.2 18.1 %all-to-all-start = ((bf16[32,32,128]{2,1,0:T(8,128)(2,1)}), bf16[32,32,128]{2,1,0:T(8,128)(2,1)S(1)}, u32[]{:S(2)}, u32[]{:S(2)}) async-start(bf16[32,32,128]{2,1,0:T(8,128)(2,1)} %get-tuple-element.15), calls=%async_computation | async-start | bytes 524288 | tf_op jit(solution)/shard_map/all_to_all | solution.py:499
  10.5 6.1 %collective-permute-start = (f32[256,128]{1,0:T(8,128)}, f32[256,128]{1,0:T(8,128)S(1)}, u32[]{:S(2)}, u32[]{:S(2)}) collective-permute-start(f32[256,128]{1,0:T(8,128)} %get-tuple-element.17), channel_id=1, source_target_pairs={{0,1},{1,0},{2,3},{3,2},{4,5},{5,4},{6,7},{7,6},{8,9},{9,8},{10,11... | collective-permute-start | bytes 393224 | tf_op jit(solution)/shard_map/ppermute | solution.py:500
  10.8 5.8 %collective-permute-start.1 = (f32[256,128]{1,0:T(8,128)}, f32[256,128]{1,0:T(8,128)S(1)}, u32[]{:S(2)}, u32[]{:S(2)}) collective-permute-start(f32[256,128]{1,0:T(8,128)} %get-tuple-element.18), channel_id=1, source_target_pairs={{1,2},{3,4},{5,6},{7,8},{9,10},{11,12},{13,14},{2,1},{4,3},{6,5},{... | collective-permute-start | bytes 393224 | tf_op jit(solution)/shard_map/ppermute | solution.py:502
  11.5 5.2 %copy-start.3 = (f32[1,16]{1,0:T(1,128)S(1)}, f32[1,16]{1,0:T(1,128)}, u32[]{:S(2)}) copy-start(f32[1,16]{1,0:T(1,128)} %param.14) | copy-start | bytes 196
  11.5 5.9 %copy-start = (f32[1,16,16]{2,1,0:T(8,128)S(1)}, f32[1,16,16]{2,1,0:T(8,128)}, u32[]{:S(2)}) copy-start(f32[1,16,16]{2,1,0:T(8,128)} %param.15) | copy-start | bytes 3076
  16.6 0.7 %copy-start.1 = (f32[256,128]{1,0:T(8,128)}, f32[256,128]{1,0:T(8,128)S(1)}, u32[]{:S(2)}) copy-start(f32[256,128]{1,0:T(8,128)S(1)} %collective-permute-done.from_a_in) | copy-start | bytes 393220
  16.7 0.7 %copy-start.2 = (f32[256,128]{1,0:T(8,128)}, f32[256,128]{1,0:T(8,128)S(1)}, u32[]{:S(2)}) copy-start(f32[256,128]{1,0:T(8,128)S(1)} %collective-permute-done.1.from_b_in) | copy-start | bytes 393220
  25.8 17.7 %all-to-all-start.1 = ((bf16[32,32,128]{2,1,0:T(8,128)(2,1)}), bf16[32,32,128]{2,1,0:T(8,128)(2,1)S(1)}, u32[]{:S(2)}, u32[]{:S(2)}) async-start(bf16[32,32,128]{2,1,0:T(8,128)(2,1)} %get-tuple-element.26), calls=%async_computation.1 | async-start | bytes 524288 | tf_op jit(solution)/shard_map/all_to_all | solution.py:531

commit v3 on v2

v3 whole, which is shorter than its diff:
```python
import functools

import jax
import jax.numpy as jnp
from jax import lax
from jax.experimental import pallas as pl
from jax.experimental.pallas import tpu as pltpu
from jax.sharding import PartitionSpec as P


NF = 8
BLK = 128
CAP = 4
NSUB = 2
SUB = 8
F32 = jnp.float32
BF16 = jnp.bfloat16
VMEM_LIMIT = 12 * 1024 * 1024


def tile_view(grid):
    levels, rows, cells = grid.shape
    split = grid.reshape(levels, rows // SUB, SUB, cells // BLK, BLK)
    return split.transpose(0, 1, 3, 2, 4).reshape(levels * rows * cells // BLK, BLK)


def from_tile_view(tiles, levels, rows, cells):
    split = tiles.reshape(levels, rows // SUB, cells // BLK, SUB, BLK)
    return split.transpose(0, 1, 3, 2, 4).reshape(levels, rows, cells)


def tile_row(row, x, columns):
    return (lax.div(row, SUB) * columns + x) * SUB + lax.rem(row, SUB)


def block_tile_row(block, columns):
    return tile_row(lax.div(block, columns), lax.rem(block, columns), columns)


def aligned(index, step):
    return pl.multiple_of(index * step, step)


def loop(count, body, unroll=1):
    def step(i, carry):
        body(i)
        return carry

    lax.fori_loop(0, count, step, 0, unroll=min(unroll, count))


class Copies:
    def __init__(self, semaphores):
        self.semaphores, self.open, self.used = semaphores, {}, 0

    def start(self, name, source, target):
        copy = pltpu.make_async_copy(source, target, self.semaphores.at[self.used])
        self.used += 1
        copy.start()
        self.open[name] = copy

    def wait(self, *names):
        for name in names:
            self.open.pop(name).wait()

    def wait_all(self):
        self.wait(*list(self.open))


def parts_of(count, parts):
    parts = parts if count % parts == 0 else 1
    return [pl.ds(i * (count // parts), count // parts) for i in range(parts)]


def pick_kernel(dims, src_in, state_in, sent_out, slab_a, slab_b, src, state, sent, sems):
    rows, columns, levels, tiles = dims
    copies = Copies(sems)
    level_stride = rows * columns
    copies.start("src", src_in, src)
    for i, part in enumerate(parts_of(NF * level_stride, 4)):
        copies.start(("top", i), state_in.at[part], state.at[part])
    deep = pl.ds(NF * level_stride, (levels - NF) * level_stride)
    copies.start("deep", state_in.at[deep], state.at[deep])
    comp, tile = lax.axis_index("comp"), lax.axis_index("tile")
    other = (1 - comp) * tiles

    def blank(t):
        sent[comp * tiles + t] = jnp.zeros((CAP * NF, BLK), BF16)

    loop(tiles, blank, unroll=16)

    def one_tile(t):
        for pair in range(CAP // 2):
            two = []
            for k in (2 * pair, 2 * pair + 1):
                start = block_tile_row(src[k, t], columns)
                two.append(state[pl.ds(start, NF, stride=level_stride), :])
            both = jnp.concatenate(two, axis=0).astype(BF16)
            sent[other + t, pl.ds(2 * NF * pair, 2 * NF), :] = both

    copies.wait("src", *[("top", i) for i in range(len(parts_of(NF * level_stride, 4)))])
    loop(tiles, one_tile, unroll=16)
    for name, half in (("sent", other), ("own", comp * tiles)):
        where = pl.ds(half, tiles)
        copies.start(name, sent.at[where], sent_out.at[where])
    even = lax.rem(tile, 2) == 0
    copies.wait("deep")
    for slab, first in (
        (slab_a, jnp.where(even, rows - NSUB, 0)),
        (slab_b, jnp.where(even, 0, rows - NSUB)),
    ):
        for i in range(NSUB):
            for x in range(columns):
                start = tile_row(first + i, x, columns)
                value = state[pl.ds(start, levels, stride=level_stride), :]
                slab[(i * columns + x) * levels : (i * columns + x + 1) * levels, :] = value.astype(BF16)
    copies.wait_all()


def row_of(ref, r, columns, levels):
    return [ref[pl.ds(aligned(r * columns + x, levels), levels), :] for x in range(columns)]


def put_row(ref, r, values, columns, levels):
    for x, v in enumerate(values):
        ref[pl.ds(aligned(r * columns + x, levels), levels), :] = v


def stencil(rate, up, mid, down):
    columns = len(mid)
    keep = 1.0 - 4.0 * rate
    lane = lax.broadcasted_iota(jnp.int32, rate.shape, 1)
    right_roll = [pltpu.roll(v, 1, 1) for v in mid]
    left_roll = [pltpu.roll(v, BLK - 1, 1) for v in mid]
    out = []
    for x in range(columns):
        west = jnp.where(lane == 0, right_roll[x - 1], right_roll[x])
        east = jnp.where(lane == BLK - 1, left_roll[(x + 1) % columns], left_roll[x])
        out.append(keep * mid[x] + rate * (up[x] + down[x] + (west + east)))
    return out


def mixing_of(col_mix):
    mix_high = col_mix.astype(BF16)
    mix_low = (col_mix - mix_high.astype(F32)).astype(BF16)
    return jnp.concatenate([mix_high, mix_high, mix_low], axis=1)


def column_physics(diffused, mixing, land):
    whole = jnp.concatenate(diffused, axis=1)
    high = whole.astype(BF16)
    low = (whole - high.astype(F32)).astype(BF16)
    three = jnp.concatenate([high, low, high], axis=0)
    moved = whole + 0.5 * jnp.tanh(jnp.dot(mixing, three, preferred_element_type=F32))
    top = moved[:NF] - (0.5 * (1.0 - land)) * whole[:NF]
    columns = len(diffused)
    cut = lambda v: [v[:, x * BLK : (x + 1) * BLK] for x in range(columns)]
    return cut(top), cut(moved[NF:])


def inner_kernel(
    dims, kappa, state_in, mask_in, mix_in, weight_in, near, base_out, deep_out, mask_edge, mix, weight,
    mask, state, blocks, stepped, base, deep, sems,
):
    rows, columns, levels, _ = dims
    depth = levels - NF
    copies = Copies(sems)
    level_stride = rows * columns
    parts = parts_of(rows // SUB, 4)
    for i, part in enumerate(parts):
        where = pl.ds(part.start * columns * SUB, part.size * columns * SUB)
        copies.start(i, state_in.at[:, where], state.at[:, where])
    copies.start("mask", mask_in, mask)
    copies.start("mix", mix_in, mix)
    copies.start("weight", weight_in, weight)
    flat = state.reshape(levels * level_stride, BLK)
    rate = kappa[...]

    def one_row(r):
        put_row(
            blocks, r,
            [flat[pl.ds(tile_row(r, x, columns), levels, stride=level_stride), :] for x in range(columns)],
            columns, levels,
        )

    def first_step(r):
        around = [row_of(blocks, r + i, columns, levels) for i in (-1, 0, 1)]
        put_row(stepped, r, stencil(rate, *around), columns, levels)

    done = 1
    for i, part in enumerate(parts):
        copies.wait(i)
        first, size = part.start * SUB, part.size * SUB
        loop(size, lambda r, first=first: one_row(first + r), unroll=size)
        last = first + size - 1
        loop(last - done, lambda r, done=done: first_step(done + r), unroll=last - done)
        done = last
    for i, r in enumerate((0, 1, rows - 2, rows - 1)):
        put_row(near, i, row_of(blocks, r, columns, levels), columns, levels)
    for i, r in enumerate((1, 2, rows - 3, rows - 2)):
        put_row(near, 4 + i, row_of(stepped, r, columns, levels), columns, levels)
    copies.wait("mask", "mix")
    for i, r in enumerate((0, 1, rows - 2, rows - 1)):
        mask_edge[i : i + 1, :] = mask[0, r : r + 1, :]
    mixing = mixing_of(mix[...])

    def second_step(i):
        r = i + 2
        around = [row_of(stepped, r + j, columns, levels) for j in (-1, 0, 1)]
        land = mask[0, pl.ds(r, 1), :].astype(F32)
        top, rest = column_physics(stencil(rate, *around), mixing, land)
        put_row(base, r, top, columns, NF)
        put_row(deep, r, rest, columns, depth)

    loop(rows - 4, second_step, unroll=28)
    for name, source, target, size in (("base", base, base_out, NF), ("deep", deep, deep_out, depth)):
        middle = pl.ds(2 * columns * size, (rows - 4) * columns * size)
        copies.start(name, source.at[middle], target.at[middle])
    copies.wait_all()


def edge_kernel(dims, kappa, near, mask_edge, mix, from_a, from_b, base_edge, deep, stepped, sems):
    _, columns, levels, tiles = dims
    tile = lax.axis_index("tile")
    even = lax.rem(tile, 2) == 0
    above_in = jnp.where(tile > 0, 1.0, 0.0).astype(F32)
    below_in = jnp.where(tile < tiles - 1, 1.0, 0.0).astype(F32)
    rate = kappa[...]
    mixing = mixing_of(mix[...])

    def slab_row(above, i):
        first, second = (from_b, from_a) if above else (from_a, from_b)
        return [
            jnp.where(even, p.astype(F32), q.astype(F32))
            for p, q in zip(
                row_of(first, i, columns, levels), row_of(second, i, columns, levels), strict=True
            )
        ]

    old = [row_of(near, i, columns, levels) for i in range(4)]
    above = [slab_row(True, i) for i in range(NSUB)]
    below = [slab_row(False, i) for i in range(NSUB)]
    new = [
        [v * above_in for v in stencil(rate, above[0], above[1], old[0])],
        stencil(rate, above[1], old[0], old[1]),
        stencil(rate, old[2], old[3], below[0]),
        [v * below_in for v in stencil(rate, old[3], below[0], below[1])],
    ]
    for i, values in enumerate(new):
        put_row(stepped, i, values, columns, levels)
    new = lambda i: row_of(stepped, i, columns, levels)
    at = lambda i: row_of(near, 4 + i, columns, levels)
    for i, around in enumerate(
        (
            (new(0), new(1), at(0)),
            (new(1), at(0), at(1)),
            (at(2), at(3), new(2)),
            (at(3), new(2), new(3)),
        )
    ):
        land = mask_edge[i : i + 1, :].astype(F32)
        top, rest = column_physics(stencil(rate, *around), mixing, land)
        put_row(base_edge, i, top, columns, NF)
        put_row(deep, i, rest, columns, levels - NF)


def surface_kernel(
    dims, arrived, base_edge, deep_edge, weight_in, dst_in, live_in_in, src_in, live_out_in, base_in, lagged_in, mask_in, weight_out_in,
    sent_out, top_out, flux_out, deep_edge_out,
    dst, live_in, src, live_out, base, lagged, mask, weight_out, sent, top, flux,
    numerator, denominator, sems,
):
    rows, columns, _, tiles = dims
    copies = Copies(sems)
    copies.start("dst", dst_in, dst)
    copies.start("live_in", live_in_in, live_in)
    tile_parts = parts_of(tiles, 4)
    middle = pl.ds(2 * columns * NF, (rows - 4) * columns * NF)
    copies.start("base", base_in.at[middle], base.at[middle])
    copies.start("lagged", lagged_in, lagged)
    copies.start("mask", mask_in, mask)
    copies.start("src", src_in, src)
    copies.start("live_out", live_out_in, live_out)
    for i, part in enumerate(tile_parts):
        copies.start(("weight_out", i), weight_out_in.at[part], weight_out.at[part])
    copies.start("deep_edge", deep_edge, deep_edge_out)
    comp = lax.axis_index("comp")
    other, own = (1 - comp) * tiles, comp * tiles

    def clear(r):
        for x in range(columns):
            where = pl.ds(aligned(r * columns + x, NF), NF)
            numerator[where, :] = jnp.zeros((NF, BLK), F32)
            denominator[where, :] = jnp.zeros((NF, BLK), F32)

    loop(rows, clear, unroll=32)
    ones = jnp.ones((NF, BLK), F32)

    def receive(t):
        got = arrived[other + t].astype(F32)
        for k in range(CAP):
            both = jnp.concatenate([got[k * NF : (k + 1) * NF], ones], axis=0).astype(BF16)
            product = jnp.dot(both, weight_in[t, k], preferred_element_type=F32)
            live = jnp.where(k < live_in[t], 1.0, 0.0).astype(F32)
            product = product * live
            where = pl.ds(aligned(dst[k, t], NF), NF)
            numerator[where, :] += product[:NF]
            denominator[where, :] += product[NF:]

    copies.wait("dst", "live_in")
    loop(tiles, receive, unroll=16)
    copies.wait("base", "lagged", "mask")
    atmosphere = jnp.where(comp == 0, 1.0, 0.0).astype(F32)

    def one_row(r, held=base, held_row=None):
        held_row = r if held_row is None else held_row
        land_row = mask[0, pl.ds(r, 1), :].astype(F32)
        for x in range(columns):
            where = pl.ds(aligned(r * columns + x, NF), NF)
            land = land_row[:, x * BLK : (x + 1) * BLK]
            received = numerator[where, :] / jnp.maximum(denominator[where, :], 1.0)
            before = lagged[pl.ds(tile_row(r, x, columns), NF, stride=rows * columns), :]
            incoming = before * atmosphere + received
            state = held[pl.ds(aligned(held_row * columns + x, NF), NF), :] + land * incoming
            top[where, :] = state
            flux[where, :] = land * jnp.tanh(state - incoming)

    loop(rows - 4, lambda i: one_row(i + 2), unroll=28)
    for i, r in enumerate((0, 1, rows - 2, rows - 1)):
        one_row(r, base_edge, i)
    copies.start("top", top, top_out)
    copies.start("flux", flux, flux_out)

    rows_of = lax.broadcasted_iota(jnp.int32, (SUB, BLK), 0)

    def send(t):
        sums = jnp.zeros((SUB, BLK), F32)
        for pair in range(CAP // 2):
            two = []
            for k in (2 * pair, 2 * pair + 1):
                picked = flux[pl.ds(aligned(src[k, t], NF), NF), :]
                both = jnp.concatenate([picked, ones], axis=0).astype(BF16)
                product = jnp.dot(both, weight_out[t, k], preferred_element_type=F32)
                product = product * jnp.where(k < live_out[t], 1.0, 0.0).astype(F32)
                two.append(product[:NF])
                sums = jnp.where((rows_of == k) | (rows_of == k + CAP), product[NF:], sums)
            both = jnp.concatenate(two, axis=0).astype(BF16)
            sent[other + t, pl.ds(2 * NF * pair, 2 * NF), :] = both
        high = sums.astype(BF16).astype(F32)
        sums = jnp.where(rows_of < CAP, high, sums - high)
        sums = jnp.concatenate([sums, jnp.zeros((SUB, BLK), F32)], axis=0)
        sent[own + t, pl.ds(0, 2 * SUB), :] = sums.astype(BF16)
        sent[own + t, pl.ds(2 * SUB, 2 * SUB), :] = jnp.zeros((2 * SUB, BLK), BF16)

    copies.wait("src", "live_out")
    for i, part in enumerate(tile_parts):
        copies.wait(("weight_out", i))
        loop(part.size, lambda t, part=part: send(part.start + t), unroll=16)
        for half in (other, own):
            where = pl.ds(half + part.start, part.size)
            copies.start(("sent", i, half is own), sent.at[where], sent_out.at[where])
    copies.wait_all()


def write_kernel(dims, top_in, deep_in, deep_edge_in, flux_in, new_state_out, land_flux, top, deep, flux, new_state, sems):
    rows, columns, levels, _ = dims
    copies = Copies(sems)
    copies.start("top", top_in, top)
    depth = levels - NF
    row, two = columns * depth, 2 * columns * depth
    for name, source, first, target, size in (
        ("deep", deep_in, two, two, (rows - 4) * row),
        ("above", deep_edge_in, 0, 0, two),
        ("below", deep_edge_in, two, (rows - 2) * row, two),
    ):
        copies.start(name, source.at[pl.ds(first, size)], deep.at[pl.ds(target, size)])
    copies.start("flux", flux_in, flux)
    comp = lax.axis_index("comp")
    on_land = jnp.where(comp == 1, 1.0, 0.0).astype(F32)
    cut = NF * rows * columns

    def from_blocks(source, target, count, first, scale=None):
        def one(rt):
            for x in range(columns):
                for level in range(count):
                    out = ((level + first) * (rows // SUB) + rt) * columns + x
                    start = (rt * SUB * columns + x) * count + level
                    value = source[pl.ds(start, SUB, stride=columns * count), :]
                    value = value if scale is None else value * scale
                    target[pl.ds(aligned(out, SUB), SUB), :] = value

        loop(rows // SUB, one, unroll=4)

    copies.wait("top")
    from_blocks(top, new_state, NF, 0)
    copies.start("state", new_state.at[pl.ds(0, cut)], new_state_out.at[pl.ds(0, cut)])
    copies.wait("deep", "above", "below")
    from_blocks(deep, new_state, depth, NF)
    rest = pl.ds(cut, depth * rows * columns)
    copies.start("rest", new_state.at[rest], new_state_out.at[rest])
    copies.wait("flux")
    from_blocks(flux, land_flux, NF, 0, on_land)
    copies.wait_all()


def return_kernel(dims, arrived, land_flux, dst_in, fluxes_out, dst, fluxes, numerator, denominator, sems):
    rows, columns, _, tiles = dims
    copies = Copies(sems)
    copies.start("dst", dst_in, dst)
    halves = parts_of(NF * rows * columns, 2)
    for i, part in enumerate(halves):
        copies.start(i, land_flux.at[part], fluxes.at[part])
    comp = lax.axis_index("comp")
    other = (1 - comp) * tiles
    level_stride = rows * columns

    def clear(r):
        for x in range(columns):
            where = pl.ds(aligned(r * columns + x, NF), NF)
            numerator[where, :] = jnp.zeros((NF, BLK), F32)
            denominator[where, :] = jnp.zeros((NF, BLK), F32)

    loop(rows, clear, unroll=32)

    def receive(t):
        got = arrived[other + t].astype(F32)
        sums = arrived[comp * tiles + t].astype(F32)
        sums = sums[:CAP] + sums[CAP : 2 * CAP]
        for k in range(CAP):
            where = pl.ds(aligned(dst[k, t], NF), NF)
            numerator[where, :] += got[k * NF : (k + 1) * NF]
            denominator[where, :] += jnp.broadcast_to(sums[k : k + 1], (NF, BLK))

    copies.wait("dst")
    loop(tiles, receive, unroll=16)
    copies.wait_all()

    def finish(t):
        for k in range(CAP):
            block = dst[k, t]
            where = pl.ds(aligned(block, NF), NF)
            out = pl.ds(block_tile_row(block, columns), NF, stride=level_stride)
            value = numerator[where, :] / jnp.maximum(denominator[where, :], 1.0)
            fluxes[out, :] = land_flux[out, :] + value

    loop(tiles, finish, unroll=16)
    for i, part in enumerate(halves):
        copies.start(("out", i), fluxes.at[part], fluxes_out.at[part])
    copies.wait_all()


def call(kernel, operands, places, outs, scratch, copies, limit, cost):
    vmem, hbm = pl.BlockSpec(memory_space=pltpu.VMEM), pl.BlockSpec(memory_space=pltpu.HBM)
    spec = {"v": vmem, "m": vmem, "h": hbm}
    space = {"m": pltpu.VMEM, "h": pltpu.HBM}
    operands = [
        pltpu.with_memory_space_constraint(x, space[place]) if place in space else x
        for x, place in zip(operands, places, strict=True)
    ]
    return pl.pallas_call(
        kernel,
        out_shape=[out for out, _ in outs],
        in_specs=[spec[place] for place in places],
        out_specs=[spec[place] for _, place in outs],
        scratch_shapes=[*scratch, pltpu.SemaphoreType.DMA((copies,))],
        compiler_params=pltpu.CompilerParams(vmem_limit_bytes=limit),
        cost_estimate=pl.CostEstimate(flops=cost, bytes_accessed=cost // 4, transcendentals=0),
    )(*operands)


def per_device(
    state,
    kappa,
    col_mix,
    surface_mask,
    lagged_flux,
    a2l_src,
    a2l_dst,
    a2l_count,
    a2l_weight,
    l2a_src,
    l2a_dst,
    l2a_count,
    l2a_weight,
):
    fields = state[0]
    levels, rows, cells = fields.shape
    columns = cells // BLK
    nblocks = rows * columns
    tiles = lax.axis_size("tile")
    dims = (rows, columns, levels, tiles)
    shape, vmem, smem = pltpu.HBM, pltpu.VMEM, pltpu.SMEM
    kernel = lambda f: functools.partial(f, dims)
    limit = VMEM_LIMIT + 4 * tiles * CAP * BLK * BLK
    state_tiles = tile_view(fields)
    slab = (NSUB * columns * levels, BLK)
    parcel = (2 * tiles, CAP * NF, BLK)
    top_shape = (nblocks * NF, BLK)
    deep_shape = (nblocks * (levels - NF), BLK)
    full_shape = (nblocks * levels, BLK)
    weight_shape = (tiles, CAP, BLK, BLK)
    slots, counts = smem((CAP, tiles), jnp.int32), smem((tiles,), jnp.int32)
    sent, slab_a, slab_b = call(
        kernel(pick_kernel), [a2l_src[:, 0, :].T, state_tiles], "hh",
        [(shape(parcel, BF16), "h"), (vmem(slab, BF16), "v"), (vmem(slab, BF16), "v")],
        [slots, vmem(full_shape, F32), vmem(parcel, BF16)],
        8, limit, 4_000_000,
    )
    arrived = lax.all_to_all(sent, ("comp", "tile"), split_axis=0, concat_axis=0, tiled=True)
    from_a = lax.ppermute(slab_a, "tile", [(i, i ^ 1) for i in range(tiles)])
    pairs = [(i, i + 1) for i in range(1, tiles - 1, 2)]
    from_b = lax.ppermute(slab_b, "tile", pairs + [(j, i) for i, j in pairs])
    rates = jnp.broadcast_to(kappa[0][:, None], (levels, BLK))
    near, base, deep, mask_edge, mix, weight_in = call(
        kernel(inner_kernel),
        [rates, state_tiles.reshape(levels, nblocks, BLK), surface_mask, col_mix[0], a2l_weight[0]], "vhhhh",
        [(vmem((8 * columns * levels, BLK), F32), "v"), (shape(top_shape, F32), "h"),
         (shape(deep_shape, F32), "h"), (vmem((4, cells), jnp.int32), "v"),
         (vmem((levels, levels), F32), "v"), (vmem(weight_shape, BF16), "v")],
        [vmem((1, rows, cells), jnp.int32), vmem((levels, nblocks, BLK), F32), vmem(full_shape, F32),
         vmem(full_shape, F32), vmem(top_shape, F32), vmem(deep_shape, F32)],
        9, limit, 20_000_000,
    )
    base_edge, deep_near = call(
        kernel(edge_kernel), [rates, near, mask_edge, mix, from_a, from_b], "vvvvvv",
        [(vmem((4 * columns * NF, BLK), F32), "v"), (vmem((4 * columns * (levels - NF), BLK), F32), "v")],
        [vmem((4 * columns * levels, BLK), F32)],
        1, limit, 4_000_000,
    )
    sent_back, top, flux, deep_edge = call(
        kernel(surface_kernel),
        [arrived, base_edge, deep_near, weight_in, a2l_dst[0].T, a2l_count[0], l2a_src[:, 0, :].T,
         l2a_count[:, 0], base, tile_view(lagged_flux), surface_mask, l2a_weight[:, 0]], "vvvvhhhhhhhh",
        [(shape(parcel, BF16), "h"), (shape(top_shape, F32), "h"), (shape(top_shape, F32), "h"),
         (shape((4 * columns * (levels - NF), BLK), F32), "h")],
        [slots, counts, slots, counts, vmem(top_shape, F32), vmem(top_shape, F32), vmem((1, rows, cells), jnp.int32),
         vmem(weight_shape, BF16), vmem(parcel, BF16), vmem(top_shape, F32), vmem(top_shape, F32), vmem(top_shape, F32), vmem(top_shape, F32)],
        23, limit, 20_000_000,
    )
    returned = lax.all_to_all(
        sent_back, ("comp", "tile"), split_axis=0, concat_axis=0, tiled=True
    )
    new_state, land_flux = call(
        kernel(write_kernel), [top, deep, deep_edge, flux], "hhhh",
        [(shape(full_shape, F32), "h"), (vmem(top_shape, F32), "v")],
        [vmem(top_shape, F32), vmem(deep_shape, F32), vmem(top_shape, F32), vmem(full_shape, F32),
         ],
        8, limit, 20_000_000,
    )
    (fluxes,) = call(
        kernel(return_kernel), [returned, land_flux, l2a_dst[0].T], "vvh",
        [(shape(top_shape, F32), "h")],
        [slots, vmem(top_shape, F32), vmem(top_shape, F32), vmem(top_shape, F32)],
        6, limit, 10_000_000,
    )
    return (
        from_tile_view(new_state, levels, rows, cells)[None],
        from_tile_view(fluxes, NF, rows, cells)[None],
    )


def solution(mesh):
    return jax.shard_map(
        per_device,
        mesh=mesh,
        in_specs=(
            P("comp", None, "tile", None),
            P("comp", None),
            P("comp", None, None),
            P("comp", "tile", None),
            P(None, "tile", None),
            P(None, "tile", None),
            P("tile", None, None),
            P("tile", None),
            P("tile", None, None, None, None),
            P(None, "tile", None),
            P("tile", None, None),
            P(None, "tile"),
            P(None, "tile", None, None, None),
        ),
        out_specs=(P("comp", None, "tile", None), P("comp", None, "tile", None)),
        check_vma=False,
    )
```

time: 46.9 us -> 42.3 us (0.902)
  Pallas kernels: 23.2 us -> 18.6 us
  waiting for transfers between devices: 6.15 us -> 10 us
  starting transfers between devices: 15.8 us -> 12.5 us
  local copies, waits for them, and re-layouts: 0.69 us -> 0.07 us
    pallas_call x6, Pallas kernels: 23.2 us -> 18.6 us  [call(): pl.pallas_call(kernel, out_shape=[out for out, _ in outs], in_specs=[spec...]
    all_to_all x1, waiting for transfers between devices: 0.01 us -> 3.27 us  [per_device(): lax.all_to_all(sent, ('comp', 'tile'), split_axis=0, concat_axis=0, tiled...]
    all_to_all x1, starting transfers between devices: 7.47 us -> 4.23 us  [per_device(): lax.all_to_all(sent_back, ('comp', 'tile'), split_axis=0, concat_axis=0,...]
    unnamed x8 -> x2, local copies, waits for them, and re-layouts: 0.62 us -> 0.01 us
    all_to_all x1, waiting for transfers between devices: 6.14 us -> 6.75 us  [per_device(): lax.all_to_all(sent_back, ('comp', 'tile'), split_axis=0, concat_axis=0,...]
  transfers between devices with their start and end apart: 4 -> 4, of which waited for: 1 -> 2; matrix products, arithmetic and copies ran while one was open for 0% -> 0% of each run, Pallas kernels for 28% -> 22%
where the time goes in v3:
time: 42.3 us; the launch traced here: 42 us
  Pallas kernels  18.6 us (44%)
  starting transfers between devices  12.5 us (30%)
  waiting for transfers between devices  10 us (24%)
  between operations  0.73 us (2%)
    pallas_call x6, Pallas kernels, call(): pl.pallas_call(kernel, out_shape=[out for out, _ in outs], in_specs=[spec...  18.6 us
    all_to_all x1, starting transfers between devices, per_device(): lax.all_to_all(sent, ('comp', 'tile'), split_axis=0, concat_axis=0, tiled...  7.33 us
    all_to_all x1, waiting for transfers between devices, per_device(): lax.all_to_all(sent_back, ('comp', 'tile'), split_axis=0, concat_axis=0,...  6.75 us
    all_to_all x1, starting transfers between devices, per_device(): lax.all_to_all(sent_back, ('comp', 'tile'), split_axis=0, concat_axis=0,...  4.23 us
    all_to_all x1, waiting for transfers between devices, per_device(): lax.all_to_all(sent, ('comp', 'tile'), split_axis=0, concat_axis=0, tiled...  3.27 us
  transfers between devices with their start and end apart: 4, of which 2 were waited for; matrix products, arithmetic and copies ran while one was open for 0% of the time, Pallas kernels for 22%

profile of v3, /device:TPU:0, one launch (start us, length us, event | category | flops | bytes accessed | tf_op | source)
XLA Modules:
  0.0 42.0 jit_solution(2774319876002366728)
XLA Ops:
  0.6 0.0 copy-start
  0.6 2.4 %shard_map.140 = (bf16[32,32,128]{2,1,0:T(8,128)(2,1)}, bf16[256,128]{1,0:T(8,128)(2,1)S(1)}, bf16[256,128]{1,0:T(8,128)(2,1)S(1)}) custom-call(s32[4,16]{1,0:T(4,128)} %bitcast.49, f32[4096,128]{1,0:T(8,128)} %bitcast.40), custom_call_target="tpu_custom_call" | custom-call | flops 4000000 | bytes 1000000 | tf_op jit(solution)/shard_map/pallas_call | solution.py:460
  3.0 7.3 %all-to-all-start = ((bf16[32,32,128]{2,1,0:T(8,128)(2,1)}), bf16[32,32,128]{2,1,0:T(8,128)(2,1)S(1)}, u32[]{:S(2)}, u32[]{:S(2)}) async-start(bf16[32,32,128]{2,1,0:T(8,128)(2,1)} %get-tuple-element.19), calls=%async_computation | async-start | bytes 524288 | tf_op jit(solution)/shard_map/all_to_all | solution.py:509
  10.4 0.3 collective-permute-start
  10.7 0.7 %collective-permute-start.1 = (bf16[256,128]{1,0:T(8,128)(2,1)S(1)}, bf16[256,128]{1,0:T(8,128)(2,1)S(1)}, u32[]{:S(2)}, u32[]{:S(2)}) collective-permute-start(bf16[256,128]{1,0:T(8,128)(2,1)S(1)} %get-tuple-element.24), channel_id=1, source_target_pairs={{1,2},{3,4},{5,6},{7,8},{9,10},{11,12},{13,14},{2,1},{4,3},{6,5},{... | collective-permute-start | bytes 196616 | tf_op jit(solution)/shard_map/ppermute | solution.py:512
  11.4 0.0 copy-done
  11.4 0.1 broadcast_in_dim.8.kappa
  11.4 5.4 %shard_map.141 = (f32[1024,128]{1,0:T(8,128)S(1)}, f32[2048,128]{1,0:T(8,128)}, f32[2048,128]{1,0:T(8,128)}, s32[4,1024]{1,0:T(4,128)S(1)}, f32[16,16]{1,0:T(8,128)S(1)}, /*index=5*/bf16[16,4,128,128]{3,2,1,0:T(8,128)(2,1)S(1)}) custom-call(f32[16,128]{1,0:T(8,128)S(1)} %broadcast_in_dim.8.kappa, f32[16,256,128]{2,1,0:T(8,128)} %bitcast.41, ...), custom_call_target="tpu_custom_call" | custom-call | flops 20000000 | bytes 5000000 | tf_op jit(solution)/shard_map/pallas_call | solution.py:460
  16.8 0.0 collective-permute-done.from_a
  16.8 0.0 collective-permute-done.1.from_b
  16.8 0.5 %shard_map.142 = (f32[256,128]{1,0:T(8,128)S(1)}, f32[256,128]{1,0:T(8,128)S(1)}) custom-call(f32[16,128]{1,0:T(8,128)S(1)} %broadcast_in_dim.8.kappa, f32[1024,128]{1,0:T(8,128)S(1)} %get-tuple-element.20.near, s32[4,1024]{1,0:T(4,128)S(1)} %get-tuple-element.21.mask_edge, f32[16,16]{1,0:T(8,128)S(1)} %get-tuple-element.22.mix, ...), custom_call_target="tpu_custom_call" | custom-call | flops 4000000 | bytes 1000000 | tf_op jit(solution)/shard_map/pallas_call | solution.py:460
  17.4 3.3 %all-to-all-done.arrived = bf16[32,32,128]{2,1,0:T(8,128)(2,1)S(1)} async-done(((bf16[32,32,128]{2,1,0:T(8,128)(2,1)}), bf16[32,32,128]{2,1,0:T(8,128)(2,1)S(1)}, u32[]{:S(2)}, u32[]{:S(2)}) %all-to-all-start) | async-done | bytes 262176 | tf_op jit(solution)/shard_map/all_to_all | solution.py:509
  20.6 4.4 %shard_map.143 = (bf16[32,32,128]{2,1,0:T(8,128)(2,1)}, f32[2048,128]{1,0:T(8,128)}, f32[2048,128]{1,0:T(8,128)}, f32[256,128]{1,0:T(8,128)}) custom-call(bf16[32,32,128]{2,1,0:T(8,128)(2,1)S(1)} %all-to-all-done.arrived, f32[256,128]{1,0:T(8,128)S(1)} %get-tuple-element.25.base_edge, f32[256,128]{1,0:T(8,128)S(1)} %get-tuple-element.26.deep_edge, ...), custom_call_target="tpu_custom_call" | custom-call | flops 20000000 | bytes 5000000 | tf_op jit(solution)/shard_map/pallas_call | solution.py:460
  25.0 4.2 %all-to-all-start.1 = ((bf16[32,32,128]{2,1,0:T(8,128)(2,1)}), bf16[32,32,128]{2,1,0:T(8,128)(2,1)S(1)}, u32[]{:S(2)}, u32[]{:S(2)}) async-start(bf16[32,32,128]{2,1,0:T(8,128)(2,1)} %get-tuple-element.34), calls=%async_computation.1 | async-start | bytes 524288 | tf_op jit(solution)/shard_map/all_to_all | solution.py:540
  29.2 3.5 %shard_map.144 = (f32[4096,128]{1,0:T(8,128)}, f32[2048,128]{1,0:T(8,128)S(1)}) custom-call(f32[2048,128]{1,0:T(8,128)} %get-tuple-element.29.top_in, f32[2048,128]{1,0:T(8,128)} %get-tuple-element.30.deep_in, f32[256,128]{1,0:T(8,128)} %get-tuple-element.31.deep_edge_in, f32[2048,128]{1,0:T(8,128)} %get-tuple-element.32.flux_in), custom_call_target="tpu_custom_call" | custom-call | flops 20000000 | bytes 5000000 | tf_op jit(solution)/shard_map/pallas_call | solution.py:460
  32.7 6.8 %all-to-all-done.1.arrived = bf16[32,32,128]{2,1,0:T(8,128)(2,1)S(1)} async-done(((bf16[32,32,128]{2,1,0:T(8,128)(2,1)}), bf16[32,32,128]{2,1,0:T(8,128)(2,1)S(1)}, u32[]{:S(2)}, u32[]{:S(2)}) %all-to-all-start.1) | async-done | bytes 262176 | tf_op jit(solution)/shard_map/all_to_all | solution.py:540
  39.5 2.5 %shard_map.145 = f32[2048,128]{1,0:T(8,128)} custom-call(bf16[32,32,128]{2,1,0:T(8,128)(2,1)S(1)} %all-to-all-done.1.arrived, f32[2048,128]{1,0:T(8,128)S(1)} %get-tuple-element.35.land_flux, s32[4,16]{1,0:T(4,128)} %bitcast.50), custom_call_target="tpu_custom_call" | custom-call | flops 10000000 | bytes 2500000 | tf_op jit(solution)/shard_map/pallas_call | solution.py:460
Async XLA Ops:
  0.6 10.7 %copy-start = (f32[1,16]{1,0:T(1,128)S(1)}, f32[1,16]{1,0:T(1,128)}, u32[]{:S(2)}) copy-start(f32[1,16]{1,0:T(1,128)} %param.14) | copy-start | bytes 196
  3.0 17.6 %all-to-all-start = ((bf16[32,32,128]{2,1,0:T(8,128)(2,1)}), bf16[32,32,128]{2,1,0:T(8,128)(2,1)S(1)}, u32[]{:S(2)}, u32[]{:S(2)}) async-start(bf16[32,32,128]{2,1,0:T(8,128)(2,1)} %get-tuple-element.19), calls=%async_computation | async-start | bytes 524288 | tf_op jit(solution)/shard_map/all_to_all | solution.py:509
  10.4 6.5 %collective-permute-start = (bf16[256,128]{1,0:T(8,128)(2,1)S(1)}, bf16[256,128]{1,0:T(8,128)(2,1)S(1)}, u32[]{:S(2)}, u32[]{:S(2)}) collective-permute-start(bf16[256,128]{1,0:T(8,128)(2,1)S(1)} %get-tuple-element.23), channel_id=1, source_target_pairs={{0,1},{1,0},{2,3},{3,2},{4,5},{5,4},{6,7},{7,6},{8,9},{9,8},{10,11... | collective-permute-start | bytes 196616 | tf_op jit(solution)/shard_map/ppermute | solution.py:510
  10.7 6.1 %collective-permute-start.1 = (bf16[256,128]{1,0:T(8,128)(2,1)S(1)}, bf16[256,128]{1,0:T(8,128)(2,1)S(1)}, u32[]{:S(2)}, u32[]{:S(2)}) collective-permute-start(bf16[256,128]{1,0:T(8,128)(2,1)S(1)} %get-tuple-element.24), channel_id=1, source_target_pairs={{1,2},{3,4},{5,6},{7,8},{9,10},{11,12},{13,14},{2,1},{4,3},{6,5},{... | collective-permute-start | bytes 196616 | tf_op jit(solution)/shard_map/ppermute | solution.py:512
  25.0 14.5 %all-to-all-start.1 = ((bf16[32,32,128]{2,1,0:T(8,128)(2,1)}), bf16[32,32,128]{2,1,0:T(8,128)(2,1)S(1)}, u32[]{:S(2)}, u32[]{:S(2)}) async-start(bf16[32,32,128]{2,1,0:T(8,128)(2,1)} %get-tuple-element.34), calls=%async_computation.1 | async-start | bytes 524288 | tf_op jit(solution)/shard_map/all_to_all | solution.py:540

commit v4 on v3

--- a/solution.py
+++ b/solution.py
@@ -212,10 +212,11 @@
         put_row(base, r, top, columns, NF)
         put_row(deep, r, rest, columns, depth)
 
-    loop(rows - 4, second_step, unroll=28)
-    for name, source, target, size in (("base", base, base_out, NF), ("deep", deep, deep_out, depth)):
-        middle = pl.ds(2 * columns * size, (rows - 4) * columns * size)
-        copies.start(name, source.at[middle], target.at[middle])
+    for first, last in ((0, rows - 20), (rows - 20, rows - 10), (rows - 10, rows - 4)):
+        loop(last - first, lambda i, first=first: second_step(first + i), unroll=28)
+        for name, source, target, size in (("base", base, base_out, NF), ("deep", deep, deep_out, depth)):
+            middle = pl.ds((2 + first) * columns * size, (last - first) * columns * size)
+            copies.start((name, first), source.at[middle], target.at[middle])
     copies.wait_all()
 
 
@@ -353,8 +354,8 @@
         sent[own + t, pl.ds(2 * SUB, 2 * SUB), :] = jnp.zeros((2 * SUB, BLK), BF16)
 
     copies.wait("src", "live_out")
-    for i, part in enumerate(tile_parts):
-        copies.wait(("weight_out", i))
+    copies.wait(*[("weight_out", i) for i in range(len(tile_parts))])
+    for i, part in enumerate(parts_of(tiles, 2)):
         loop(part.size, lambda t, part=part: send(part.start + t), unroll=16)
         for half in (other, own):
             where = pl.ds(half + part.start, part.size)
@@ -519,7 +520,7 @@
          (vmem((levels, levels), F32), "v"), (vmem(weight_shape, BF16), "v")],
         [vmem((1, rows, cells), jnp.int32), vmem((levels, nblocks, BLK), F32), vmem(full_shape, F32),
          vmem(full_shape, F32), vmem(top_shape, F32), vmem(deep_shape, F32)],
-        9, limit, 20_000_000,
+        16, limit, 20_000_000,
     )
     base_edge, deep_near = call(
         kernel(edge_kernel), [rates, near, mask_edge, mix, from_a, from_b], "vvvvvv",
@@ -548,7 +549,7 @@
         8, limit, 20_000_000,
     )
     (fluxes,) = call(
-        kernel(return_kernel), [returned, land_flux, l2a_dst[0].T], "vvh",
+        kernel(return_kernel), [returned, land_flux, l2a_dst[0].T], "vvm",
         [(shape(top_shape, F32), "h")],
         [slots, vmem(top_shape, F32), vmem(top_shape, F32), vmem(top_shape, F32)],
         6, limit, 10_000_000,

time: 42.3 us -> 41.5 us (0.981)
  Pallas kernels: 18.6 us -> 17.8 us
    pallas_call x6, Pallas kernels: 18.6 us -> 17.8 us  [call(): pl.pallas_call(kernel, out_shape=[out for out, _ in outs], in_specs=[spec...]
    all_to_all x1, starting transfers between devices: 4.23 us -> 3.8 us  [per_device(): lax.all_to_all(sent_back, ('comp', 'tile'), split_axis=0, concat_axis=0,...]
where the time goes in v4:
time: 41.5 us; the launch traced here: 41.1 us
  Pallas kernels  17.8 us (43%)
  starting transfers between devices  12.1 us (29%)
  waiting for transfers between devices  10.4 us (25%)
  between operations  0.74 us (2%)
    pallas_call x6, Pallas kernels, call(): pl.pallas_call(kernel, out_shape=[out for out, _ in outs], in_specs=[spec...  17.8 us
    all_to_all x1, starting transfers between devices, per_device(): lax.all_to_all(sent, ('comp', 'tile'), split_axis=0, concat_axis=0, tiled...  7.33 us
    all_to_all x1, waiting for transfers between devices, per_device(): lax.all_to_all(sent_back, ('comp', 'tile'), split_axis=0, concat_axis=0,...  6.75 us
    all_to_all x1, starting transfers between devices, per_device(): lax.all_to_all(sent_back, ('comp', 'tile'), split_axis=0, concat_axis=0,...  3.8 us
    all_to_all x1, waiting for transfers between devices, per_device(): lax.all_to_all(sent, ('comp', 'tile'), split_axis=0, concat_axis=0, tiled...  3.68 us
  transfers between devices with their start and end apart: 4, of which 2 were waited for; matrix products, arithmetic and copies ran while one was open for 0% of the time, Pallas kernels for 22%

profile of v4, /device:TPU:0, one launch (start us, length us, event | category | flops | bytes accessed | tf_op | source)
XLA Modules:
  0.0 41.1 jit_solution(11241403255676894124)
XLA Ops:
  0.6 0.0 copy-start.1
  0.6 2.4 %shard_map.140 = (bf16[32,32,128]{2,1,0:T(8,128)(2,1)}, bf16[256,128]{1,0:T(8,128)(2,1)S(1)}, bf16[256,128]{1,0:T(8,128)(2,1)S(1)}) custom-call(s32[4,16]{1,0:T(4,128)} %bitcast.50, f32[4096,128]{1,0:T(8,128)} %bitcast.41), custom_call_target="tpu_custom_call" | custom-call | flops 4000000 | bytes 1000000 | tf_op jit(solution)/shard_map/pallas_call | solution.py:461
  3.0 7.3 %all-to-all-start = ((bf16[32,32,128]{2,1,0:T(8,128)(2,1)}), bf16[32,32,128]{2,1,0:T(8,128)(2,1)S(1)}, u32[]{:S(2)}, u32[]{:S(2)}) async-start(bf16[32,32,128]{2,1,0:T(8,128)(2,1)} %get-tuple-element.19), calls=%async_computation | async-start | bytes 524288 | tf_op jit(solution)/shard_map/all_to_all | solution.py:510
  10.4 0.3 collective-permute-start
  10.7 0.7 %collective-permute-start.1 = (bf16[256,128]{1,0:T(8,128)(2,1)S(1)}, bf16[256,128]{1,0:T(8,128)(2,1)S(1)}, u32[]{:S(2)}, u32[]{:S(2)}) collective-permute-start(bf16[256,128]{1,0:T(8,128)(2,1)S(1)} %get-tuple-element.24), channel_id=1, source_target_pairs={{1,2},{3,4},{5,6},{7,8},{9,10},{11,12},{13,14},{2,1},{4,3},{6,5},{... | collective-permute-start | bytes 196616 | tf_op jit(solution)/shard_map/ppermute | solution.py:513
  11.4 0.0 copy-done.1
  11.4 0.1 broadcast_in_dim.8.kappa
  11.4 5.0 %shard_map.141 = (f32[1024,128]{1,0:T(8,128)S(1)}, f32[2048,128]{1,0:T(8,128)}, f32[2048,128]{1,0:T(8,128)}, s32[4,1024]{1,0:T(4,128)S(1)}, f32[16,16]{1,0:T(8,128)S(1)}, /*index=5*/bf16[16,4,128,128]{3,2,1,0:T(8,128)(2,1)S(1)}) custom-call(f32[16,128]{1,0:T(8,128)S(1)} %broadcast_in_dim.8.kappa, f32[16,256,128]{2,1,0:T(8,128)} %bitcast.42, ...), custom_call_target="tpu_custom_call" | custom-call | flops 20000000 | bytes 5000000 | tf_op jit(solution)/shard_map/pallas_call | solution.py:461
  16.4 0.0 collective-permute-done.from_a
  16.4 0.0 collective-permute-done.1.from_b
  16.4 0.5 %shard_map.142 = (f32[256,128]{1,0:T(8,128)S(1)}, f32[256,128]{1,0:T(8,128)S(1)}) custom-call(f32[16,128]{1,0:T(8,128)S(1)} %broadcast_in_dim.8.kappa, f32[1024,128]{1,0:T(8,128)S(1)} %get-tuple-element.20.near, s32[4,1024]{1,0:T(4,128)S(1)} %get-tuple-element.21.mask_edge, f32[16,16]{1,0:T(8,128)S(1)} %get-tuple-element.22.mix, ...), custom_call_target="tpu_custom_call" | custom-call | flops 4000000 | bytes 1000000 | tf_op jit(solution)/shard_map/pallas_call | solution.py:461
  16.9 3.7 %all-to-all-done.arrived = bf16[32,32,128]{2,1,0:T(8,128)(2,1)S(1)} async-done(((bf16[32,32,128]{2,1,0:T(8,128)(2,1)}), bf16[32,32,128]{2,1,0:T(8,128)(2,1)S(1)}, u32[]{:S(2)}, u32[]{:S(2)}) %all-to-all-start) | async-done | bytes 262176 | tf_op jit(solution)/shard_map/all_to_all | solution.py:510
  20.6 4.0 %shard_map.143 = (bf16[32,32,128]{2,1,0:T(8,128)(2,1)}, f32[2048,128]{1,0:T(8,128)}, f32[2048,128]{1,0:T(8,128)}, f32[256,128]{1,0:T(8,128)}) custom-call(bf16[32,32,128]{2,1,0:T(8,128)(2,1)S(1)} %all-to-all-done.arrived, f32[256,128]{1,0:T(8,128)S(1)} %get-tuple-element.25.base_edge, f32[256,128]{1,0:T(8,128)S(1)} %get-tuple-element.26.deep_edge, ...), custom_call_target="tpu_custom_call" | custom-call | flops 20000000 | bytes 5000000 | tf_op jit(solution)/shard_map/pallas_call | solution.py:461
  24.7 0.0 copy-start
  24.7 3.8 %all-to-all-start.1 = ((bf16[32,32,128]{2,1,0:T(8,128)(2,1)}), bf16[32,32,128]{2,1,0:T(8,128)(2,1)S(1)}, u32[]{:S(2)}, u32[]{:S(2)}) async-start(bf16[32,32,128]{2,1,0:T(8,128)(2,1)} %get-tuple-element.34), calls=%async_computation.1 | async-start | bytes 524288 | tf_op jit(solution)/shard_map/all_to_all | solution.py:541
  28.5 3.5 %shard_map.144 = (f32[4096,128]{1,0:T(8,128)}, f32[2048,128]{1,0:T(8,128)S(1)}) custom-call(f32[2048,128]{1,0:T(8,128)} %get-tuple-element.29.top_in, f32[2048,128]{1,0:T(8,128)} %get-tuple-element.30.deep_in, f32[256,128]{1,0:T(8,128)} %get-tuple-element.31.deep_edge_in, f32[2048,128]{1,0:T(8,128)} %get-tuple-element.32.flux_in), custom_call_target="tpu_custom_call" | custom-call | flops 20000000 | bytes 5000000 | tf_op jit(solution)/shard_map/pallas_call | solution.py:461
  32.0 6.8 %all-to-all-done.1.arrived = bf16[32,32,128]{2,1,0:T(8,128)(2,1)S(1)} async-done(((bf16[32,32,128]{2,1,0:T(8,128)(2,1)}), bf16[32,32,128]{2,1,0:T(8,128)(2,1)S(1)}, u32[]{:S(2)}, u32[]{:S(2)}) %all-to-all-start.1) | async-done | bytes 262176 | tf_op jit(solution)/shard_map/all_to_all | solution.py:541
  38.7 0.0 copy-done
  38.7 2.4 %shard_map.145 = f32[2048,128]{1,0:T(8,128)} custom-call(bf16[32,32,128]{2,1,0:T(8,128)(2,1)S(1)} %all-to-all-done.1.arrived, f32[2048,128]{1,0:T(8,128)S(1)} %get-tuple-element.35.land_flux, s32[4,16]{1,0:T(4,128)S(1)} %bitcast.40), custom_call_target="tpu_custom_call" | custom-call | flops 10000000 | bytes 2500000 | tf_op jit(solution)/shard_map/pallas_call | solution.py:461
Async XLA Ops:
  0.6 10.7 %copy-start.1 = (f32[1,16]{1,0:T(1,128)S(1)}, f32[1,16]{1,0:T(1,128)}, u32[]{:S(2)}) copy-start(f32[1,16]{1,0:T(1,128)} %param.14) | copy-start | bytes 196
  3.0 17.6 %all-to-all-start = ((bf16[32,32,128]{2,1,0:T(8,128)(2,1)}), bf16[32,32,128]{2,1,0:T(8,128)(2,1)S(1)}, u32[]{:S(2)}, u32[]{:S(2)}) async-start(bf16[32,32,128]{2,1,0:T(8,128)(2,1)} %get-tuple-element.19), calls=%async_computation | async-start | bytes 524288 | tf_op jit(solution)/shard_map/all_to_all | solution.py:510
  10.4 6.0 %collective-permute-start = (bf16[256,128]{1,0:T(8,128)(2,1)S(1)}, bf16[256,128]{1,0:T(8,128)(2,1)S(1)}, u32[]{:S(2)}, u32[]{:S(2)}) collective-permute-start(bf16[256,128]{1,0:T(8,128)(2,1)S(1)} %get-tuple-element.23), channel_id=1, source_target_pairs={{0,1},{1,0},{2,3},{3,2},{4,5},{5,4},{6,7},{7,6},{8,9},{9,8},{10,11... | collective-permute-start | bytes 196616 | tf_op jit(solution)/shard_map/ppermute | solution.py:511
  10.7 5.7 %collective-permute-start.1 = (bf16[256,128]{1,0:T(8,128)(2,1)S(1)}, bf16[256,128]{1,0:T(8,128)(2,1)S(1)}, u32[]{:S(2)}, u32[]{:S(2)}) collective-permute-start(bf16[256,128]{1,0:T(8,128)(2,1)S(1)} %get-tuple-element.24), channel_id=1, source_target_pairs={{1,2},{3,4},{5,6},{7,8},{9,10},{11,12},{13,14},{2,1},{4,3},{6,5},{... | collective-permute-start | bytes 196616 | tf_op jit(solution)/shard_map/ppermute | solution.py:513
  24.7 14.1 %copy-start = (s32[1,16,4]{1,2,0:T(4,128)S(1)}, s32[1,16,4]{1,2,0:T(4,128)}, u32[]{:S(2)}) copy-start(s32[1,16,4]{1,2,0:T(4,128)} %param.23) | copy-start | bytes 772
  24.7 14.1 %all-to-all-start.1 = ((bf16[32,32,128]{2,1,0:T(8,128)(2,1)}), bf16[32,32,128]{2,1,0:T(8,128)(2,1)S(1)}, u32[]{:S(2)}, u32[]{:S(2)}) async-start(bf16[32,32,128]{2,1,0:T(8,128)(2,1)} %get-tuple-element.34), calls=%async_computation.1 | async-start | bytes 524288 | tf_op jit(solution)/shard_map/all_to_all | solution.py:541

commit v5 on v4

--- a/solution.py
+++ b/solution.py
@@ -121,6 +121,17 @@
     return [ref[pl.ds(aligned(r * columns + x, levels), levels), :] for x in range(columns)]
 
 
+def rows_of_tile(ref, rt, x, columns, level_stride, levels):
+    tall = []
+    for half in range(levels // SUB):
+        tiles = []
+        for level in range(half * SUB, (half + 1) * SUB):
+            start = pl.multiple_of(level * level_stride + (rt * columns + x) * SUB, SUB)
+            tiles.append(ref[pl.ds(start, SUB), :])
+        tall.append(jnp.transpose(jnp.stack(tiles), (1, 0, 2)))
+    return [jnp.concatenate([t[i] for t in tall], axis=0) for i in range(SUB)]
+
+
 def put_row(ref, r, values, columns, levels):
     for x, v in enumerate(values):
         ref[pl.ds(aligned(r * columns + x, levels), levels), :] = v
@@ -176,12 +187,11 @@
     flat = state.reshape(levels * level_stride, BLK)
     rate = kappa[...]
 
-    def one_row(r):
-        put_row(
-            blocks, r,
-            [flat[pl.ds(tile_row(r, x, columns), levels, stride=level_stride), :] for x in range(columns)],
-            columns, levels,
-        )
+    def one_tile_row(rt):
+        for x in range(columns):
+            for i, value in enumerate(rows_of_tile(flat, rt, x, columns, level_stride, levels)):
+                where = (rt * SUB + i) * columns + x
+                blocks[pl.ds(aligned(where, levels), levels), :] = value
 
     def first_step(r):
         around = [row_of(blocks, r + i, columns, levels) for i in (-1, 0, 1)]
@@ -191,7 +201,7 @@
     for i, part in enumerate(parts):
         copies.wait(i)
         first, size = part.start * SUB, part.size * SUB
-        loop(size, lambda r, first=first: one_row(first + r), unroll=size)
+        loop(part.size, lambda rt, part=part: one_tile_row(part.start + rt), unroll=part.size)
         last = first + size - 1
         loop(last - done, lambda r, done=done: first_step(done + r), unroll=last - done)
         done = last
@@ -310,8 +320,17 @@
 
     copies.wait("dst", "live_in")
     loop(tiles, receive, unroll=16)
-    copies.wait("base", "lagged", "mask")
+    copies.wait("lagged")
     atmosphere = jnp.where(comp == 0, 1.0, 0.0).astype(F32)
+
+    def earlier(rt):
+        for x in range(columns):
+            for i, value in enumerate(rows_of_tile(lagged, rt, x, columns, rows * columns, NF)):
+                where = (rt * SUB + i) * columns + x
+                top[pl.ds(aligned(where, NF), NF), :] = value * atmosphere
+
+    loop(rows // SUB, earlier, unroll=4)
+    copies.wait("base", "mask")
 
     def one_row(r, held=base, held_row=None):
         held_row = r if held_row is None else held_row
@@ -320,8 +339,7 @@
             where = pl.ds(aligned(r * columns + x, NF), NF)
             land = land_row[:, x * BLK : (x + 1) * BLK]
             received = numerator[where, :] / jnp.maximum(denominator[where, :], 1.0)
-            before = lagged[pl.ds(tile_row(r, x, columns), NF, stride=rows * columns), :]
-            incoming = before * atmosphere + received
+            incoming = top[where, :] + received
             state = held[pl.ds(aligned(held_row * columns + x, NF), NF), :] + land * incoming
             top[where, :] = state
             flux[where, :] = land * jnp.tanh(state - incoming)

time: 41.5 us -> 41 us (0.988)
  Pallas kernels: 17.8 us -> 17.3 us
    pallas_call x6, Pallas kernels: 17.8 us -> 17.3 us  [call(): pl.pallas_call(kernel, out_shape=[out for out, _ in outs], in_specs=[spec...]
  transfers between devices with their start and end apart: 4 -> 4, of which waited for: 2 -> 2; matrix products, arithmetic and copies ran while one was open for 0% -> 0% of each run, Pallas kernels for 22% -> 21%
where the time goes in v5:
time: 41 us; the launch traced here: 40.7 us
  Pallas kernels  17.3 us (42%)
  starting transfers between devices  11.9 us (29%)
  waiting for transfers between devices  10.7 us (26%)
  between operations  0.74 us (2%)
    pallas_call x6, Pallas kernels, call(): pl.pallas_call(kernel, out_shape=[out for out, _ in outs], in_specs=[spec...  17.3 us
    all_to_all x1, starting transfers between devices, per_device(): lax.all_to_all(sent, ('comp', 'tile'), split_axis=0, concat_axis=0, tiled...  7.33 us
    all_to_all x1, waiting for transfers between devices, per_device(): lax.all_to_all(sent_back, ('comp', 'tile'), split_axis=0, concat_axis=0,...  6.75 us
    all_to_all x1, waiting for transfers between devices, per_device(): lax.all_to_all(sent, ('comp', 'tile'), split_axis=0, concat_axis=0, tiled...  3.91 us
    all_to_all x1, starting transfers between devices, per_device(): lax.all_to_all(sent_back, ('comp', 'tile'), split_axis=0, concat_axis=0,...  3.58 us
  transfers between devices with their start and end apart: 4, of which 2 were waited for; matrix products, arithmetic and copies ran while one was open for 0% of the time, Pallas kernels for 21%

profile of v5, /device:TPU:0, one launch (start us, length us, event | category | flops | bytes accessed | tf_op | source)
XLA Modules:
  0.0 40.7 jit_solution(9994482483633361719)
XLA Ops:
  0.6 0.0 copy-start.1
  0.6 2.4 %shard_map.140 = (bf16[32,32,128]{2,1,0:T(8,128)(2,1)}, bf16[256,128]{1,0:T(8,128)(2,1)S(1)}, bf16[256,128]{1,0:T(8,128)(2,1)S(1)}) custom-call(s32[4,16]{1,0:T(4,128)} %bitcast.50, f32[4096,128]{1,0:T(8,128)} %bitcast.41), custom_call_target="tpu_custom_call" | custom-call | flops 4000000 | bytes 1000000 | tf_op jit(solution)/shard_map/pallas_call | solution.py:479
  3.0 7.3 %all-to-all-start = ((bf16[32,32,128]{2,1,0:T(8,128)(2,1)}), bf16[32,32,128]{2,1,0:T(8,128)(2,1)S(1)}, u32[]{:S(2)}, u32[]{:S(2)}) async-start(bf16[32,32,128]{2,1,0:T(8,128)(2,1)} %get-tuple-element.19), calls=%async_computation | async-start | bytes 524288 | tf_op jit(solution)/shard_map/all_to_all | solution.py:528
  10.4 0.3 collective-permute-start
  10.7 0.7 %collective-permute-start.1 = (bf16[256,128]{1,0:T(8,128)(2,1)S(1)}, bf16[256,128]{1,0:T(8,128)(2,1)S(1)}, u32[]{:S(2)}, u32[]{:S(2)}) collective-permute-start(bf16[256,128]{1,0:T(8,128)(2,1)S(1)} %get-tuple-element.24), channel_id=1, source_target_pairs={{1,2},{3,4},{5,6},{7,8},{9,10},{11,12},{13,14},{2,1},{4,3},{6,5},{... | collective-permute-start | bytes 196616 | tf_op jit(solution)/shard_map/ppermute | solution.py:531
  11.4 0.0 copy-done.1
  11.4 0.1 broadcast_in_dim.8.kappa
  11.4 4.7 %shard_map.141 = (f32[1024,128]{1,0:T(8,128)S(1)}, f32[2048,128]{1,0:T(8,128)}, f32[2048,128]{1,0:T(8,128)}, s32[4,1024]{1,0:T(4,128)S(1)}, f32[16,16]{1,0:T(8,128)S(1)}, /*index=5*/bf16[16,4,128,128]{3,2,1,0:T(8,128)(2,1)S(1)}) custom-call(f32[16,128]{1,0:T(8,128)S(1)} %broadcast_in_dim.8.kappa, f32[16,256,128]{2,1,0:T(8,128)} %bitcast.42, ...), custom_call_target="tpu_custom_call" | custom-call | flops 20000000 | bytes 5000000 | tf_op jit(solution)/shard_map/pallas_call | solution.py:479
  16.2 0.0 collective-permute-done.from_a
  16.2 0.0 collective-permute-done.1.from_b
  16.2 0.5 %shard_map.142 = (f32[256,128]{1,0:T(8,128)S(1)}, f32[256,128]{1,0:T(8,128)S(1)}) custom-call(f32[16,128]{1,0:T(8,128)S(1)} %broadcast_in_dim.8.kappa, f32[1024,128]{1,0:T(8,128)S(1)} %get-tuple-element.20.near, s32[4,1024]{1,0:T(4,128)S(1)} %get-tuple-element.21.mask_edge, f32[16,16]{1,0:T(8,128)S(1)} %get-tuple-element.22.mix, ...), custom_call_target="tpu_custom_call" | custom-call | flops 4000000 | bytes 1000000 | tf_op jit(solution)/shard_map/pallas_call | solution.py:479
  16.7 3.9 %all-to-all-done.arrived = bf16[32,32,128]{2,1,0:T(8,128)(2,1)S(1)} async-done(((bf16[32,32,128]{2,1,0:T(8,128)(2,1)}), bf16[32,32,128]{2,1,0:T(8,128)(2,1)S(1)}, u32[]{:S(2)}, u32[]{:S(2)}) %all-to-all-start) | async-done | bytes 262176 | tf_op jit(solution)/shard_map/all_to_all | solution.py:528
  20.6 3.8 %shard_map.143 = (bf16[32,32,128]{2,1,0:T(8,128)(2,1)}, f32[2048,128]{1,0:T(8,128)}, f32[2048,128]{1,0:T(8,128)}, f32[256,128]{1,0:T(8,128)}) custom-call(bf16[32,32,128]{2,1,0:T(8,128)(2,1)S(1)} %all-to-all-done.arrived, f32[256,128]{1,0:T(8,128)S(1)} %get-tuple-element.25.base_edge, f32[256,128]{1,0:T(8,128)S(1)} %get-tuple-element.26.deep_edge, ...), custom_call_target="tpu_custom_call" | custom-call | flops 20000000 | bytes 5000000 | tf_op jit(solution)/shard_map/pallas_call | solution.py:479
  24.4 0.0 copy-start
  24.4 3.6 %all-to-all-start.1 = ((bf16[32,32,128]{2,1,0:T(8,128)(2,1)}), bf16[32,32,128]{2,1,0:T(8,128)(2,1)S(1)}, u32[]{:S(2)}, u32[]{:S(2)}) async-start(bf16[32,32,128]{2,1,0:T(8,128)(2,1)} %get-tuple-element.34), calls=%async_computation.1 | async-start | bytes 524288 | tf_op jit(solution)/shard_map/all_to_all | solution.py:559
  28.0 3.5 %shard_map.144 = (f32[4096,128]{1,0:T(8,128)}, f32[2048,128]{1,0:T(8,128)S(1)}) custom-call(f32[2048,128]{1,0:T(8,128)} %get-tuple-element.29.top_in, f32[2048,128]{1,0:T(8,128)} %get-tuple-element.30.deep_in, f32[256,128]{1,0:T(8,128)} %get-tuple-element.31.deep_edge_in, f32[2048,128]{1,0:T(8,128)} %get-tuple-element.32.flux_in), custom_call_target="tpu_custom_call" | custom-call | flops 20000000 | bytes 5000000 | tf_op jit(solution)/shard_map/pallas_call | solution.py:479
  31.5 6.8 %all-to-all-done.1.arrived = bf16[32,32,128]{2,1,0:T(8,128)(2,1)S(1)} async-done(((bf16[32,32,128]{2,1,0:T(8,128)(2,1)}), bf16[32,32,128]{2,1,0:T(8,128)(2,1)S(1)}, u32[]{:S(2)}, u32[]{:S(2)}) %all-to-all-start.1) | async-done | bytes 262176 | tf_op jit(solution)/shard_map/all_to_all | solution.py:559
  38.3 0.0 copy-done
  38.3 2.4 %shard_map.145 = f32[2048,128]{1,0:T(8,128)} custom-call(bf16[32,32,128]{2,1,0:T(8,128)(2,1)S(1)} %all-to-all-done.1.arrived, f32[2048,128]{1,0:T(8,128)S(1)} %get-tuple-element.35.land_flux, s32[4,16]{1,0:T(4,128)S(1)} %bitcast.40), custom_call_target="tpu_custom_call" | custom-call | flops 10000000 | bytes 2500000 | tf_op jit(solution)/shard_map/pallas_call | solution.py:479
Async XLA Ops:
  0.6 10.7 %copy-start.1 = (f32[1,16]{1,0:T(1,128)S(1)}, f32[1,16]{1,0:T(1,128)}, u32[]{:S(2)}) copy-start(f32[1,16]{1,0:T(1,128)} %param.14) | copy-start | bytes 196
  3.0 17.6 %all-to-all-start = ((bf16[32,32,128]{2,1,0:T(8,128)(2,1)}), bf16[32,32,128]{2,1,0:T(8,128)(2,1)S(1)}, u32[]{:S(2)}, u32[]{:S(2)}) async-start(bf16[32,32,128]{2,1,0:T(8,128)(2,1)} %get-tuple-element.19), calls=%async_computation | async-start | bytes 524288 | tf_op jit(solution)/shard_map/all_to_all | solution.py:528
  10.4 5.8 %collective-permute-start = (bf16[256,128]{1,0:T(8,128)(2,1)S(1)}, bf16[256,128]{1,0:T(8,128)(2,1)S(1)}, u32[]{:S(2)}, u32[]{:S(2)}) collective-permute-start(bf16[256,128]{1,0:T(8,128)(2,1)S(1)} %get-tuple-element.23), channel_id=1, source_target_pairs={{0,1},{1,0},{2,3},{3,2},{4,5},{5,4},{6,7},{7,6},{8,9},{9,8},{10,11... | collective-permute-start | bytes 196616 | tf_op jit(solution)/shard_map/ppermute | solution.py:529
  10.7 5.5 %collective-permute-start.1 = (bf16[256,128]{1,0:T(8,128)(2,1)S(1)}, bf16[256,128]{1,0:T(8,128)(2,1)S(1)}, u32[]{:S(2)}, u32[]{:S(2)}) collective-permute-start(bf16[256,128]{1,0:T(8,128)(2,1)S(1)} %get-tuple-element.24), channel_id=1, source_target_pairs={{1,2},{3,4},{5,6},{7,8},{9,10},{11,12},{13,14},{2,1},{4,3},{6,5},{... | collective-permute-start | bytes 196616 | tf_op jit(solution)/shard_map/ppermute | solution.py:531
  24.4 13.9 %copy-start = (s32[1,16,4]{1,2,0:T(4,128)S(1)}, s32[1,16,4]{1,2,0:T(4,128)}, u32[]{:S(2)}) copy-start(s32[1,16,4]{1,2,0:T(4,128)} %param.23) | copy-start | bytes 772
  24.4 13.8 %all-to-all-start.1 = ((bf16[32,32,128]{2,1,0:T(8,128)(2,1)}), bf16[32,32,128]{2,1,0:T(8,128)(2,1)S(1)}, u32[]{:S(2)}, u32[]{:S(2)}) async-start(bf16[32,32,128]{2,1,0:T(8,128)(2,1)} %get-tuple-element.34), calls=%async_computation.1 | async-start | bytes 524288 | tf_op jit(solution)/shard_map/all_to_all | solution.py:559

commit v6 on v5

--- a/solution.py
+++ b/solution.py
@@ -381,7 +381,7 @@
     copies.wait_all()
 
 
-def write_kernel(dims, top_in, deep_in, deep_edge_in, flux_in, new_state_out, land_flux, top, deep, flux, new_state, sems):
+def write_kernel(dims, top_in, deep_in, deep_edge_in, flux_in, new_state_out, land_flux, land_blocks, top, deep, flux, new_state, sems):
     rows, columns, levels, _ = dims
     copies = Copies(sems)
     copies.start("top", top_in, top)
@@ -419,14 +419,15 @@
     copies.start("rest", new_state.at[rest], new_state_out.at[rest])
     copies.wait("flux")
     from_blocks(flux, land_flux, NF, 0, on_land)
+    land_blocks[...] = flux[...] * on_land
     copies.wait_all()
 
 
-def return_kernel(dims, arrived, land_flux, dst_in, fluxes_out, dst, fluxes, numerator, denominator, sems):
+def return_kernel(dims, arrived, land_flux, land_blocks, dst_in, fluxes_out, dst, fluxes, numerator, denominator, sems):
     rows, columns, _, tiles = dims
     copies = Copies(sems)
     copies.start("dst", dst_in, dst)
-    halves = parts_of(NF * rows * columns, 2)
+    halves = parts_of(NF * rows * columns, 1)
     for i, part in enumerate(halves):
         copies.start(i, land_flux.at[part], fluxes.at[part])
     comp = lax.axis_index("comp")
@@ -460,7 +461,7 @@
             where = pl.ds(aligned(block, NF), NF)
             out = pl.ds(block_tile_row(block, columns), NF, stride=level_stride)
             value = numerator[where, :] / jnp.maximum(denominator[where, :], 1.0)
-            fluxes[out, :] = land_flux[out, :] + value
+            fluxes[out, :] = land_blocks[where, :] + value
 
     loop(tiles, finish, unroll=16)
     for i, part in enumerate(halves):
@@ -559,15 +560,15 @@
     returned = lax.all_to_all(
         sent_back, ("comp", "tile"), split_axis=0, concat_axis=0, tiled=True
     )
-    new_state, land_flux = call(
+    new_state, land_flux, land_blocks = call(
         kernel(write_kernel), [top, deep, deep_edge, flux], "hhhh",
-        [(shape(full_shape, F32), "h"), (vmem(top_shape, F32), "v")],
+        [(shape(full_shape, F32), "h"), (vmem(top_shape, F32), "v"), (vmem(top_shape, F32), "v")],
         [vmem(top_shape, F32), vmem(deep_shape, F32), vmem(top_shape, F32), vmem(full_shape, F32),
          ],
         8, limit, 20_000_000,
     )
     (fluxes,) = call(
-        kernel(return_kernel), [returned, land_flux, l2a_dst[0].T], "vvm",
+        kernel(return_kernel), [returned, land_flux, land_blocks, l2a_dst[0].T], "vvvm",
         [(shape(top_shape, F32), "h")],
         [slots, vmem(top_shape, F32), vmem(top_shape, F32), vmem(top_shape, F32)],
         6, limit, 10_000_000,

time: 41 us -> 41 us (level)
  transfers between devices with their start and end apart: 4 -> 4, of which waited for: 2 -> 2; matrix products, arithmetic and copies ran while one was open for 0% -> 0% of each run, Pallas kernels for 21% -> 22%
where the time goes in v6:
time: 41 us; the launch traced here: 40.6 us
  Pallas kernels  17.3 us (42%)
  starting transfers between devices  11.9 us (29%)
  waiting for transfers between devices  10.7 us (26%)
  between operations  0.74 us (2%)
    pallas_call x6, Pallas kernels, call(): pl.pallas_call(kernel, out_shape=[out for out, _ in outs], in_specs=[spec...  17.3 us
    all_to_all x1, starting transfers between devices, per_device(): lax.all_to_all(sent, ('comp', 'tile'), split_axis=0, concat_axis=0, tiled...  7.33 us
    all_to_all x1, waiting for transfers between devices, per_device(): lax.all_to_all(sent_back, ('comp', 'tile'), split_axis=0, concat_axis=0,...  6.75 us
    all_to_all x1, waiting for transfers between devices, per_device(): lax.all_to_all(sent, ('comp', 'tile'), split_axis=0, concat_axis=0, tiled...  3.91 us
    all_to_all x1, starting transfers between devices, per_device(): lax.all_to_all(sent_back, ('comp', 'tile'), split_axis=0, concat_axis=0,...  3.58 us
  transfers between devices with their start and end apart: 4, of which 2 were waited for; matrix products, arithmetic and copies ran while one was open for 0% of the time, Pallas kernels for 22%

profile of v6, /device:TPU:0, one launch (start us, length us, event | category | flops | bytes accessed | tf_op | source)
XLA Modules:
  0.0 40.6 jit_solution(2173909501750364949)
XLA Ops:
  0.6 0.0 copy-start.1
  0.6 2.4 %shard_map.140 = (bf16[32,32,128]{2,1,0:T(8,128)(2,1)}, bf16[256,128]{1,0:T(8,128)(2,1)S(1)}, bf16[256,128]{1,0:T(8,128)(2,1)S(1)}) custom-call(s32[4,16]{1,0:T(4,128)} %bitcast.50, f32[4096,128]{1,0:T(8,128)} %bitcast.41), custom_call_target="tpu_custom_call" | custom-call | flops 4000000 | bytes 1000000 | tf_op jit(solution)/shard_map/pallas_call | solution.py:480
  3.0 7.3 %all-to-all-start = ((bf16[32,32,128]{2,1,0:T(8,128)(2,1)}), bf16[32,32,128]{2,1,0:T(8,128)(2,1)S(1)}, u32[]{:S(2)}, u32[]{:S(2)}) async-start(bf16[32,32,128]{2,1,0:T(8,128)(2,1)} %get-tuple-element.20), calls=%async_computation | async-start | bytes 524288 | tf_op jit(solution)/shard_map/all_to_all | solution.py:529
  10.4 0.3 collective-permute-start
  10.7 0.7 %collective-permute-start.1 = (bf16[256,128]{1,0:T(8,128)(2,1)S(1)}, bf16[256,128]{1,0:T(8,128)(2,1)S(1)}, u32[]{:S(2)}, u32[]{:S(2)}) collective-permute-start(bf16[256,128]{1,0:T(8,128)(2,1)S(1)} %get-tuple-element.25), channel_id=1, source_target_pairs={{1,2},{3,4},{5,6},{7,8},{9,10},{11,12},{13,14},{2,1},{4,3},{6,5},{... | collective-permute-start | bytes 196616 | tf_op jit(solution)/shard_map/ppermute | solution.py:532
  11.4 0.0 copy-done.1
  11.4 0.1 broadcast_in_dim.8.kappa
  11.4 4.7 %shard_map.141 = (f32[1024,128]{1,0:T(8,128)S(1)}, f32[2048,128]{1,0:T(8,128)}, f32[2048,128]{1,0:T(8,128)}, s32[4,1024]{1,0:T(4,128)S(1)}, f32[16,16]{1,0:T(8,128)S(1)}, /*index=5*/bf16[16,4,128,128]{3,2,1,0:T(8,128)(2,1)S(1)}) custom-call(f32[16,128]{1,0:T(8,128)S(1)} %broadcast_in_dim.8.kappa, f32[16,256,128]{2,1,0:T(8,128)} %bitcast.42, ...), custom_call_target="tpu_custom_call" | custom-call | flops 20000000 | bytes 5000000 | tf_op jit(solution)/shard_map/pallas_call | solution.py:480
  16.2 0.0 collective-permute-done.from_a
  16.2 0.0 collective-permute-done.1.from_b
  16.2 0.5 %shard_map.142 = (f32[256,128]{1,0:T(8,128)S(1)}, f32[256,128]{1,0:T(8,128)S(1)}) custom-call(f32[16,128]{1,0:T(8,128)S(1)} %broadcast_in_dim.8.kappa, f32[1024,128]{1,0:T(8,128)S(1)} %get-tuple-element.21.near, s32[4,1024]{1,0:T(4,128)S(1)} %get-tuple-element.22.mask_edge, f32[16,16]{1,0:T(8,128)S(1)} %get-tuple-element.23.mix, ...), custom_call_target="tpu_custom_call" | custom-call | flops 4000000 | bytes 1000000 | tf_op jit(solution)/shard_map/pallas_call | solution.py:480
  16.7 3.9 %all-to-all-done.arrived = bf16[32,32,128]{2,1,0:T(8,128)(2,1)S(1)} async-done(((bf16[32,32,128]{2,1,0:T(8,128)(2,1)}), bf16[32,32,128]{2,1,0:T(8,128)(2,1)S(1)}, u32[]{:S(2)}, u32[]{:S(2)}) %all-to-all-start) | async-done | bytes 262176 | tf_op jit(solution)/shard_map/all_to_all | solution.py:529
  20.6 3.8 %shard_map.143 = (bf16[32,32,128]{2,1,0:T(8,128)(2,1)}, f32[2048,128]{1,0:T(8,128)}, f32[2048,128]{1,0:T(8,128)}, f32[256,128]{1,0:T(8,128)}) custom-call(bf16[32,32,128]{2,1,0:T(8,128)(2,1)S(1)} %all-to-all-done.arrived, f32[256,128]{1,0:T(8,128)S(1)} %get-tuple-element.26.base_edge, f32[256,128]{1,0:T(8,128)S(1)} %get-tuple-element.27.deep_edge, ...), custom_call_target="tpu_custom_call" | custom-call | flops 20000000 | bytes 5000000 | tf_op jit(solution)/shard_map/pallas_call | solution.py:480
  24.4 0.0 copy-start
  24.4 3.6 %all-to-all-start.1 = ((bf16[32,32,128]{2,1,0:T(8,128)(2,1)}), bf16[32,32,128]{2,1,0:T(8,128)(2,1)S(1)}, u32[]{:S(2)}, u32[]{:S(2)}) async-start(bf16[32,32,128]{2,1,0:T(8,128)(2,1)} %get-tuple-element.35), calls=%async_computation.1 | async-start | bytes 524288 | tf_op jit(solution)/shard_map/all_to_all | solution.py:560
  28.0 3.5 %shard_map.144 = (f32[4096,128]{1,0:T(8,128)}, f32[2048,128]{1,0:T(8,128)S(1)}, f32[2048,128]{1,0:T(8,128)S(1)}) custom-call(f32[2048,128]{1,0:T(8,128)} %get-tuple-element.30.top_in, f32[2048,128]{1,0:T(8,128)} %get-tuple-element.31.deep_in, f32[256,128]{1,0:T(8,128)} %get-tuple-element.32.deep_edge_in, f32[2048,128]{1,0:T(8,128)} %get-tuple-element.33.flux_in), custom_call_target="tpu_custom_call" | custom-call | flops 20000000 | bytes 5000000 | tf_op jit(solution)/shard_map/pallas_call | solution.py:480
  31.5 6.8 %all-to-all-done.1.arrived = bf16[32,32,128]{2,1,0:T(8,128)(2,1)S(1)} async-done(((bf16[32,32,128]{2,1,0:T(8,128)(2,1)}), bf16[32,32,128]{2,1,0:T(8,128)(2,1)S(1)}, u32[]{:S(2)}, u32[]{:S(2)}) %all-to-all-start.1) | async-done | bytes 262176 | tf_op jit(solution)/shard_map/all_to_all | solution.py:560
  38.3 0.0 copy-done
  38.3 2.4 %shard_map.145 = f32[2048,128]{1,0:T(8,128)} custom-call(bf16[32,32,128]{2,1,0:T(8,128)(2,1)S(1)} %all-to-all-done.1.arrived, f32[2048,128]{1,0:T(8,128)S(1)} %get-tuple-element.36.land_flux, f32[2048,128]{1,0:T(8,128)S(1)} %get-tuple-element.37.land_blocks, s32[4,16]{1,0:T(4,128)S(1)} %bitcast.40), custom_call_target="tpu_custom_call" | custom-call | flops 10000000 | bytes 2500000 | tf_op jit(solution)/shard_map/pallas_call | solution.py:480
Async XLA Ops:
  0.6 10.7 %copy-start.1 = (f32[1,16]{1,0:T(1,128)S(1)}, f32[1,16]{1,0:T(1,128)}, u32[]{:S(2)}) copy-start(f32[1,16]{1,0:T(1,128)} %param.14) | copy-start | bytes 196
  3.0 17.6 %all-to-all-start = ((bf16[32,32,128]{2,1,0:T(8,128)(2,1)}), bf16[32,32,128]{2,1,0:T(8,128)(2,1)S(1)}, u32[]{:S(2)}, u32[]{:S(2)}) async-start(bf16[32,32,128]{2,1,0:T(8,128)(2,1)} %get-tuple-element.20), calls=%async_computation | async-start | bytes 524288 | tf_op jit(solution)/shard_map/all_to_all | solution.py:529
  10.4 5.8 %collective-permute-start = (bf16[256,128]{1,0:T(8,128)(2,1)S(1)}, bf16[256,128]{1,0:T(8,128)(2,1)S(1)}, u32[]{:S(2)}, u32[]{:S(2)}) collective-permute-start(bf16[256,128]{1,0:T(8,128)(2,1)S(1)} %get-tuple-element.24), channel_id=1, source_target_pairs={{0,1},{1,0},{2,3},{3,2},{4,5},{5,4},{6,7},{7,6},{8,9},{9,8},{10,11... | collective-permute-start | bytes 196616 | tf_op jit(solution)/shard_map/ppermute | solution.py:530
  10.7 5.5 %collective-permute-start.1 = (bf16[256,128]{1,0:T(8,128)(2,1)S(1)}, bf16[256,128]{1,0:T(8,128)(2,1)S(1)}, u32[]{:S(2)}, u32[]{:S(2)}) collective-permute-start(bf16[256,128]{1,0:T(8,128)(2,1)S(1)} %get-tuple-element.25), channel_id=1, source_target_pairs={{1,2},{3,4},{5,6},{7,8},{9,10},{11,12},{13,14},{2,1},{4,3},{6,5},{... | collective-permute-start | bytes 196616 | tf_op jit(solution)/shard_map/ppermute | solution.py:532
  24.4 13.9 %copy-start = (s32[1,16,4]{1,2,0:T(4,128)S(1)}, s32[1,16,4]{1,2,0:T(4,128)}, u32[]{:S(2)}) copy-start(s32[1,16,4]{1,2,0:T(4,128)} %param.23) | copy-start | bytes 772
  24.4 13.8 %all-to-all-start.1 = ((bf16[32,32,128]{2,1,0:T(8,128)(2,1)}), bf16[32,32,128]{2,1,0:T(8,128)(2,1)S(1)}, u32[]{:S(2)}, u32[]{:S(2)}) async-start(bf16[32,32,128]{2,1,0:T(8,128)(2,1)} %get-tuple-element.35), calls=%async_computation.1 | async-start | bytes 524288 | tf_op jit(solution)/shard_map/all_to_all | solution.py:560
